TPU v7x, 128 devices: a whole 4x4x4 slice. The times are simulated.
128 devices in a mesh: grp: 8 (over y, core), sub: 16 (over x, z).
Axes of the slice: x: 4, y: 4, z: 4, core: 2. Of those that a mesh axis runs over, the one named last changes fastest.
Arguments:
- sources: float32 [32, 64, 16384], P(None, None, ('grp', 'sub')), may hold values from -6 to 6
- coords: float32 [3, 64, 16384], P(None, None, ('grp', 'sub')), may hold values from 0 to 2
- leaf_basis: float32 [32, 64, 16384], P(None, None, ('grp', 'sub')), may hold values from -0.75 to 0.75
- transfer: float32 [32, 32, 16384], P(None, None, ('grp', 'sub')), may hold values from -1 to 1
- send_list: int32 [2048, 16], P(('grp', 'sub')), may hold values from 0 to 127
- near_list: int32 [7, 16384], P(None, ('grp', 'sub')), may hold values from 0 to 383
- near_count: int32 [16384], P(('grp', 'sub')), may hold values from 1 to 7, as said below
- far_list: int32 [16, 2048], P(None, ('grp', 'sub')), may hold values from 0 to 255
- coupling: float32 [32, 32, 16, 2048], P(None, None, None, ('grp', 'sub')), may hold values from -0.25 to 0.25
- group_transfer: float32 [32, 32, 2048], P(None, None, ('grp', 'sub')), may hold values from -0.0625 to 0.0625
- group_coupling: float32 [32, 32, 8, 8], replicated, may hold values from -1 to 1
Outputs:
- potential: float32 [32, 64, 16384], P(None, None, ('grp', 'sub'))
Inputs may be any that keep to these rules, and one draw needn't show every extreme that they name: `near_count`: every device holds a leaf with 7 live entries; the fewest live entries differ from device to device.
All inputs are finite; a program needn't handle non-finite values.
Results may differ from a plain program's by a relative error of at most 0.0003.
Values sent between devices are 32-bit elements; how exact they have to be, the bound alone decides.
No kernel may reach another device: no remote copies, remote signals or barrier semaphores. Data moves between devices by JAX's collectives and lax.ppermute only.
A program may use at most 192 MiB of HBM per device.

v0:
```python
import math

import jax
import jax.numpy as jnp
from jax import lax
from jax.experimental import pallas as pl
from jax.experimental.pallas import tpu as pltpu
from jax.sharding import PartitionSpec as P

INV_FOUR_PI = 1.0 / (4.0 * math.pi)
EPS_SQ = 0.01
F32, BF16 = jnp.float32, jnp.bfloat16
NT = (((1,), (1,)), ((), ()))
NN = (((1,), (0,)), ((), ()))

POINTS_AT, NEAR_ROWS = 256, 280
INFLOW_AT, FAR_ROWS = 128, 136


def split(x):
    hi = x.astype(BF16)
    return hi, (x - hi.astype(F32)).astype(BF16)


def split3(x):
    hi = x.astype(BF16).astype(F32)
    rest = x - hi
    mid = rest.astype(BF16).astype(F32)
    return hi, mid, rest - mid


def mm(a, b, dims):
    return lax.dot_general(a, b, dims, preferred_element_type=F32)


def dot3(a, b, dims):
    ah, al = split(a)
    bh, bl = split(b)
    return mm(ah, bh, dims) + (mm(ah, bl, dims) + mm(al, bh, dims))


def low_half(shape):
    return lax.broadcasted_iota(jnp.int32, shape, len(shape) - 1) < 64


def rows(i, n):
    return pl.ds(pl.multiple_of(i * n, n), n)


def twice(block):
    return jnp.transpose(jnp.concatenate([block, block], 0))


def pack_kernel(send, src, crd, out, src_t, pts_t, planes):
    def source_rows(i, _):
        for r in range(4):
            planes[i * 4 + r] = twice(src[i * 4 + r])
        return 0

    lax.fori_loop(0, 8, source_rows, 0)

    def eight_leaves(g, _):
        block = jnp.transpose(planes[:, rows(g, 8), :], (1, 0, 2))
        src_t[rows(g, 256), :] = block.reshape(256, 128)
        return 0

    lax.fori_loop(0, 16, eight_leaves, 0)
    for c in range(3):
        planes[c] = twice(crd[c] - 1.0)
    for c in range(3, 8):
        planes[c] = jnp.zeros((128, 128), F32)

    def eight_points(g, _):
        block = jnp.transpose(planes[0:8, rows(g, 8), :], (1, 0, 2))
        pts_t[rows(g, 64), :] = block.reshape(64, 128)
        return 0

    lax.fori_loop(0, 16, eight_points, 0)
    low = low_half((32, 128))
    low8 = low_half((8, 128))

    def one_peer(q, _):
        for p in range(8):
            first, second = send[q, 2 * p], send[q, 2 * p + 1]
            out[q, pl.ds(32 * p, 32), :] = jnp.where(low, src_t[rows(first, 32), :], src_t[rows(second, 32), :])
            pts = jnp.where(low8, pts_t[rows(first, 8), :], pts_t[rows(second, 8), :])
            out[q, pl.ds(POINTS_AT + 3 * p, 3), :] = pts[:3]
        return 0

    lax.fori_loop(0, 16, one_peer, 0)


def upward_kernel(src_t, bas, tra, gt, wt, skel, own, gt_c, planes, w_t):
    gt_c[...] = jnp.transpose(gt[...], (1, 0, 2))

    def w_rows(jb, _):
        acc = [jnp.zeros((64, 128), F32) for _ in range(2)]
        for k in range(32):
            block = bas[k]
            for i in range(2):
                acc[i] = acc[i] + tra[jb * 2 + i, k : k + 1, :] * block
        for i in range(2):
            planes[jb * 2 + i] = twice(acc[i])
        return 0

    lax.fori_loop(0, 16, w_rows, 0)
    low = low_half((256, 128))

    def eight_leaves(g, _):
        block = jnp.transpose(planes[:, rows(g, 8), :], (1, 0, 2)).reshape(256, 128)
        w_t[rows(g, 256), :] = block
        hi = block.astype(BF16).astype(F32)
        wt[rows(g, 256), :] = jnp.where(low, hi, block - hi).astype(BF16)
        return 0

    lax.fori_loop(0, 16, eight_leaves, 0)
    low32 = low_half((32, 128))

    def one_parent(c):
        ws, ss = [], []
        for pair in range(4):
            first, second = [rows(c * 8 + pair * 2 + i, 32) for i in (0, 1)]
            w = jnp.where(low32, w_t[first, :], w_t[second, :])
            s = jnp.where(low32, src_t[first, :], src_t[second, :])
            ws.append(jnp.concatenate(split(w), 0))
            ss.append(jnp.concatenate(split(s), 0))
        total = mm(jnp.concatenate(ws, 1), jnp.concatenate(ss, 1), NT)
        both = total[:32] + total[32:]
        return both[:, :32] + both[:, 32:]

    def four_parents(cg, total):
        blocks = [one_parent(cg * 4 + i) for i in range(4)]
        skel[rows(cg, 32), :] = jnp.concatenate(blocks, 1)
        for i in range(4):
            total = total + dot3(gt_c[cg * 4 + i], blocks[i], NN)
        return total

    total = lax.fori_loop(0, 4, four_parents, jnp.zeros((32, 32), F32))
    own[...] = jnp.concatenate([total[8 * i : 8 * i + 8] for i in range(4)], 1)


def unpack(packed):
    return jnp.concatenate([packed[:, 32 * i : 32 * i + 32] for i in range(4)], 0)


def inflow_kernel(group, row, parts, skel, out):
    total = jnp.zeros((32, 32), F32)
    for m in range(1, 8):
        h = group[0] ^ m
        total = total + dot3(row[:, pl.ds(h, 1), :].reshape(32, 32), unpack(parts[m]), NN)
    packed = jnp.concatenate([total[8 * i : 8 * i + 8] for i in range(4)], 1)
    for q in range(16):
        out[q, 0:128, :] = skel[...]
        out[q, 128:136, :] = packed


def couple_kernel(cpl, out, lines):
    def one_row(k, _):
        for fg in range(4):
            lines[fg, pl.ds(k, 16, stride=32), :] = jnp.concatenate([cpl[k, 4 * fg + i] for i in range(4)], 1)
        return 0

    lax.fori_loop(0, 32, one_row, 0)

    def one_parent(c, _):
        hi, lo = split(jnp.concatenate([lines[fg, rows(c, 32), :] for fg in range(4)], 1))
        out[c, 0:32, :] = hi
        out[c, 32:64, :] = lo
        return 0

    lax.fori_loop(0, 16, one_parent, 0)


def point_rows(x, target):
    line = lax.broadcasted_iota(jnp.int32, x.shape, 0)
    norm = jnp.sum(jnp.where(line < 3, x * x, 0.0), axis=0, keepdims=True)
    if target:
        x = jnp.where(line < 3, -2.0 * x, jnp.where(line == 3, 1.0, jnp.where(line == 4, norm + EPS_SQ, 0.0)))
        a, b, c = split3(x)
        return jnp.concatenate([a, a, b, a, b, c], 0)
    x = jnp.where(line < 3, x, jnp.where(line == 3, norm, jnp.where(line == 4, 1.0, 0.0)))
    a, b, c = split3(x)
    return jnp.concatenate([a, b, a, c, b, a], 0).astype(BF16)


def put_values(ref, slot, x):
    hi, lo = split(x * INV_FOUR_PI)
    ref[slot, 0:32, :] = hi
    ref[slot, 32:64, :] = lo


def own_kernel(src_t, pts_t, vals, feats, targets):
    def some_leaves(i, _):
        for u in range(8):
            l = i * 8 + u
            put_values(vals, l, src_t[rows(l, 32), :])
            x = pts_t[rows(l, 8), :]
            feats[l] = point_rows(x, False)
            targets[l] = jnp.transpose(point_rows(x, True))[:64].astype(BF16)
        return 0

    lax.fori_loop(0, 16, some_leaves, 0)


def near_kernel(near, count, recv, targets, vals_own, feats_own, out, vals, feats, sems):
    copies = [
        pltpu.make_async_copy(vals_own, vals.at[pl.ds(0, 128)], sems.at[0]),
        pltpu.make_async_copy(feats_own, feats.at[pl.ds(0, 128)], sems.at[1]),
    ]
    for copy in copies:
        copy.start()
    vals[384] = jnp.zeros((64, 128), BF16)
    feats[384] = point_rows(jnp.zeros((8, 128), F32), False)
    low = low_half((32, 128))
    low8 = low_half((8, 128))

    def one_sender(s, _):
        for p in range(8):
            slot = 128 + s * 16 + 2 * p
            x = recv[s, pl.ds(32 * p, 32), :]
            y = pltpu.roll(x, 64, 1)
            put_values(vals, slot, jnp.where(low, x, y))
            put_values(vals, slot + 1, jnp.where(low, y, x))
            x = recv[s, pl.ds(POINTS_AT + 3 * p, 3), :]
            x = jnp.concatenate([x, jnp.zeros((5, 128), F32)], 0)
            y = pltpu.roll(x, 64, 1)
            feats[slot] = point_rows(jnp.where(low8, x, y), False)
            feats[slot + 1] = point_rows(jnp.where(low8, y, x), False)
        return 0

    lax.fori_loop(0, 16, one_sender, 0)
    for copy in copies:
        copy.wait()
    mask = low_half((64, 128))
    mask48 = low_half((48, 128))

    def one_leaf(l):
        live = count[l]
        slots = [jnp.where(e < live, near[e, l], 384) if e < 7 else 384 for e in range(8)]
        pairs = [(slots[2 * i], slots[2 * i + 1]) for i in range(4)]
        points = jnp.concatenate([jnp.where(mask48, feats[a], feats[b]) for a, b in pairs], 1)
        values = jnp.concatenate([jnp.where(mask, vals[a], vals[b]) for a, b in pairs], 1)
        kern = lax.rsqrt(mm(targets[l], points, NN))
        acc = mm(values, jnp.concatenate(split(kern), 0), NT)
        out[rows(l, 32), :] = acc[:32] + acc[32:]

    def some_leaves(i, _):
        for u in range(UNROLL):
            one_leaf(i * UNROLL + u)
        return 0

    lax.fori_loop(0, 128 // UNROLL, some_leaves, 0)


UNROLL = 4


def far_kernel(far, recv, cpl, gt_c, wt, near, out, skel, masks, planes):
    def one_sender(s, _):
        for cg in range(4):
            hi, lo = split(recv[s, pl.ds(32 * cg, 32), :])
            skel[s * 4 + cg, :, 0:128] = hi
            skel[s * 4 + cg, :, 128:256] = lo
        return 0

    lax.fori_loop(0, 16, one_sender, 0)
    lane_group = lax.broadcasted_iota(jnp.int32, (32, 256), 1) // 32 % 4
    for i in range(4):
        masks[i] = jnp.where(lane_group == i, 1.0, 0.0).astype(BF16)
    packed = recv[0, pl.ds(INFLOW_AT, 8), :]
    for s in range(1, 16):
        packed = packed + recv[s, pl.ds(INFLOW_AT, 8), :]
    inflow = unpack(packed)
    inflow_t = jnp.transpose(jnp.pad(inflow, ((0, 96), (0, 96))))[:32, :32]

    def one_parent(c):
        blocks = []
        for f in range(16):
            q = far[f, c]
            blocks.append(skel[q >> 2] * masks[q & 3])
        acc = mm(cpl[c], jnp.concatenate(blocks, 0), NN)
        both = acc[:32] + acc[32:]
        x = both[:, :128] + both[:, 128:]
        x = x + pltpu.roll(x, 64, 1)
        x = x + pltpu.roll(x, 32, 1)
        x = jnp.transpose(jnp.concatenate([x] * 4, 0))[:32, :32]
        x = x + dot3(inflow_t, gt_c[c], NN)
        field = jnp.concatenate(split(x), 0)
        leaves = []
        for i in range(8):
            acc = mm(field, wt[rows(c * 8 + i, 32), :], NN)
            leaves.append(acc[:32] + acc[32:] + near[rows(c * 8 + i, 32), :])
        planes[:, rows(c, 8), :] = jnp.transpose(jnp.stack(leaves, 0), (1, 0, 2))

    def some_parents(i, _):
        for u in range(4):
            one_parent(i * 4 + u)
        return 0

    lax.fori_loop(0, 4, some_parents, 0)

    def some_rhs(i, _):
        for u in range(4):
            x = jnp.transpose(planes[i * 4 + u])
            out[i * 4 + u] = x[:64] + x[64:]
        return 0

    lax.fori_loop(0, 8, some_rhs, 0)


VMEM = pl.BlockSpec(memory_space=pltpu.VMEM)
SMEM = pl.BlockSpec(memory_space=pltpu.SMEM)
ANY = pl.BlockSpec(memory_space=pl.ANY)


def f32(*shape):
    return jax.ShapeDtypeStruct(shape, F32)


def b16(*shape):
    return jax.ShapeDtypeStruct(shape, BF16)


def call(kernel, name, out_shape, in_specs, scratch=(), mib=56, **cost):
    several = isinstance(out_shape, tuple)
    return pl.pallas_call(
        kernel,
        out_shape=out_shape,
        in_specs=in_specs,
        out_specs=(VMEM,) * len(out_shape) if several else VMEM,
        scratch_shapes=scratch,
        compiler_params=pltpu.CompilerParams(vmem_limit_bytes=mib << 20),
        cost_estimate=pl.CostEstimate(flops=cost.get("flops", 10**9), bytes_accessed=4 << 20, transcendentals=0),
        name=name,
    )


def body(
    sources,
    coords,
    leaf_basis,
    transfer,
    send_list,
    near_list,
    near_count,
    far_list,
    coupling,
    group_transfer,
    group_coupling,
):
    planes = pltpu.VMEM((32, 128, 128), F32)
    payload, src_t, pts_t = call(
        pack_kernel,
        "pack",
        (f32(16, NEAR_ROWS, 128), f32(4096, 128), f32(1024, 128)),
        [SMEM, VMEM, VMEM],
        [planes],
    )(send_list, sources, coords)
    recv = lax.all_to_all(payload, "sub", 0, 0, tiled=True)
    wt, skel, own, gt_c = call(
        upward_kernel,
        "upward",
        (b16(4096, 128), f32(128, 128), f32(8, 128), f32(16, 32, 32)),
        [VMEM] * 4,
        [planes, pltpu.VMEM((4096, 128), F32)],
    )(src_t, leaf_basis, transfer, jnp.transpose(group_transfer, (0, 2, 1)))
    parts = own[None]
    for step in (1, 2, 4):
        other = lax.ppermute(parts, "grp", [(i, i ^ step) for i in range(8)])
        parts = jnp.concatenate([parts, other], 0)
    group = lax.axis_index("grp").astype(jnp.int32).reshape(1)
    far_payload = pl.pallas_call(
        inflow_kernel,
        out_shape=f32(16, FAR_ROWS, 128),
        grid_spec=pltpu.PrefetchScalarGridSpec(
            num_scalar_prefetch=1,
            grid=(1,),
            in_specs=[
                pl.BlockSpec((32, pl.Squeezed(), 8, 32), lambda i, g: (0, g[0], 0, 0)),
                pl.BlockSpec((8, 8, 128), lambda i, g: (0, 0, 0)),
                pl.BlockSpec((128, 128), lambda i, g: (0, 0)),
            ],
            out_specs=pl.BlockSpec((16, FAR_ROWS, 128), lambda i, g: (0, 0, 0)),
        ),
        name="inflow",
    )(group, jnp.transpose(group_coupling, (0, 2, 3, 1)), parts, skel)
    cpl = call(couple_kernel, "couple", b16(16, 64, 512), [VMEM], [pltpu.VMEM((4, 512, 128), F32)])(
        jnp.transpose(coupling, (0, 2, 3, 1))
    )
    vals_own, feats_own, targets = call(
        own_kernel, "own", (b16(128, 64, 128), b16(128, 48, 128), b16(128, 64, 48)), [VMEM] * 2
    )(src_t, pts_t)
    recv, far_payload, cpl, vals_own, feats_own, targets = lax.optimization_barrier(
        (recv, far_payload, cpl, vals_own, feats_own, targets)
    )
    far_recv = lax.all_to_all(far_payload, "sub", 0, 0, tiled=True)
    near = call(
        near_kernel,
        "near",
        f32(4096, 128),
        [SMEM] * 2 + [VMEM] * 2 + [ANY] * 2,
        [pltpu.VMEM((385, 64, 128), BF16), pltpu.VMEM((385, 48, 128), BF16), pltpu.SemaphoreType.DMA((2,))],
    )(near_list, near_count, recv, targets, vals_own, feats_own)
    return call(
        far_kernel,
        "far",
        f32(32, 64, 128),
        [SMEM] + [VMEM] * 5,
        [pltpu.VMEM((64, 32, 256), BF16), pltpu.VMEM((4, 32, 256), BF16), planes],
    )(far_list, far_recv, cpl, gt_c, wt, near)


def solution(mesh):
    leaves = P(None, None, ("grp", "sub"))
    return jax.shard_map(
        body,
        mesh=mesh,
        in_specs=(
            leaves,
            leaves,
            leaves,
            leaves,
            P(("grp", "sub"), None),
            P(None, ("grp", "sub")),
            P(("grp", "sub")),
            P(None, ("grp", "sub")),
            P(None, None, None, ("grp", "sub")),
            leaves,
            P(),
        ),
        out_specs=leaves,
        check_vma=False,
    )
```

profile of v0, /device:TPU:0, one launch (start us, length us, event | category | flops | bytes accessed | tf_op | source)
XLA Modules:
  0.0 92.3 jit_solution(1372469202331737993)
XLA Ops:
  0.0 6.0 %pack.1 = (f32[16,280,128]{2,1,0:T(8,128)}, f32[4096,128]{1,0:T(8,128)}, f32[1024,128]{1,0:T(8,128)}) custom-call(s32[16,16]{1,0:T(8,128)} %send.1, f32[32,64,128]{2,1,0:T(8,128)} %src.1, f32[3,64,128]{2,1,0:T(8,128)} %crd.1), custom_call_target="tpu_custom_call" | custom-call | flops 1000000000 | bytes 4194304 | tf_op jit(solution)/shard_map/pack/pallas_call | solution.py:352
  6.0 8.0 %all-to-all-start = ((f32[16,280,128]{2,1,0:T(8,128)}), f32[16,280,128]{2,1,0:T(8,128)S(1)}, u32[]{:S(2)}, u32[]{:S(2)}) async-start(f32[16,280,128]{2,1,0:T(8,128)} %get-tuple-element.21), calls=%async_computation | async-start | bytes 4587520 | tf_op jit(solution)/shard_map/all_to_all | solution.py:359
  14.0 9.6 %upward.1 = (bf16[4096,128]{1,0:T(8,128)(2,1)}, f32[128,128]{1,0:T(8,128)}, f32[8,128]{1,0:T(8,128)}, f32[16,32,32]{2,1,0:T(8,128)}) custom-call(f32[4096,128]{1,0:T(8,128)} %get-tuple-element.22.src_t, f32[32,64,128]{2,1,0:T(8,128)} %bas.1, f32[32,32,128]{2,1,0:T(8,128)} %tra.1, f32[32,16,32]{2,1,0:T(8,128)} %bitcast.7), custom_call_target="tpu_custom_call" | custom-call | flops 1000000000 | bytes 4194304 | tf_op jit(solution)/shard_map/upward/pallas_call | solution.py:360
  23.5 0.0 copy-start.2
  23.5 0.0 collective-permute-start
  23.5 1.4 %collective-permute-done = f32[1,8,128]{2,1,0:T(8,128)S(1)} collective-permute-done((f32[1,8,128]{2,1,0:T(8,128)}, f32[1,8,128]{2,1,0:T(8,128)S(1)}, u32[]{:S(2)}, u32[]{:S(2)}) %collective-permute-start) | collective-permute-done | bytes 4128 | tf_op jit(solution)/shard_map/ppermute | solution.py:369
  24.9 0.7 pad_maximum_fusion.2
  25.6 1.6 %collective-permute-start.1 = (f32[2,8,128]{2,1,0:T(8,128)S(1)}, f32[2,8,128]{2,1,0:T(8,128)S(1)}, u32[]{:S(2)}, u32[]{:S(2)}) collective-permute-start(f32[2,8,128]{2,1,0:T(8,128)S(1)} %pad_maximum_fusion.2), channel_id=1, source_target_pairs={{0,32},{16,48},{32,0},{48,16},{64,96},{80,112},{96,64},{112,80},{1... | collective-permute-start | bytes 24584 | tf_op jit(solution)/shard_map/ppermute | solution.py:369
  27.2 6.5 %own.1 = (bf16[128,64,128]{2,1,0:T(8,128)(2,1)}, bf16[128,48,128]{2,1,0:T(8,128)(2,1)}, bf16[128,64,48]{2,1,0:T(8,128)(2,1)}) custom-call(f32[4096,128]{1,0:T(8,128)} %get-tuple-element.22.src_t, f32[1024,128]{1,0:T(8,128)} %get-tuple-element.25.pts_t), custom_call_target="tpu_custom_call" | custom-call | flops 1000000000 | bytes 4194304 | tf_op jit(solution)/shard_map/own/pallas_call | solution.py:390
  33.6 0.0 collective-permute-done.1
  33.6 0.0 copy-done.2
  33.6 3.0 %collective-permute-start.2 = (f32[4,8,128]{2,1,0:T(8,128)S(1)}, f32[4,8,128]{2,1,0:T(8,128)S(1)}, u32[]{:S(2)}, u32[]{:S(2)}) collective-permute-start(f32[4,8,128]{2,1,0:T(8,128)S(1)} %pad_maximum_fusion.1), channel_id=1, source_target_pairs={{0,64},{16,80},{32,96},{48,112},{64,0},{80,16},{96,32},{112,48},{1... | collective-permute-start | bytes 49160 | tf_op jit(solution)/shard_map/ppermute | solution.py:369
  36.6 7.2 %couple.1.cpl = bf16[16,64,512]{2,1,0:T(8,128)(2,1)} custom-call(f32[32,16,16,32]{3,2,1,0:T(8,128)} %bitcast.5), custom_call_target="tpu_custom_call" | custom-call | flops 1000000000 | bytes 4194304 | tf_op jit(solution)/shard_map/couple/pallas_call | solution.py:387
  43.8 0.0 collective-permute-done.2
  43.8 0.6 pad_maximum_fusion.parts
  44.4 2.4 %inflow.1 = f32[16,136,128]{2,1,0:T(8,128)} custom-call(s32[1]{0:T(128)} %bitcast.group, f32[32,8,8,32]{3,2,1,0:T(8,128)} %bitcast.6, f32[8,8,128]{2,1,0:T(8,128)} %pad_maximum_fusion.parts, f32[128,128]{1,0:T(8,128)} %get-tuple-element.24.skel), custom_call_target="tpu_custom_call" | custom-call | tf_op jit(solution)/shard_map/inflow/pallas_call | solution.py:372
  46.8 0.0 all-to-all-done.recv
  46.8 0.0 copy-start
  46.9 7.2 %all-to-all-start.1 = ((f32[16,136,128]{2,1,0:T(8,128)}), f32[16,136,128]{2,1,0:T(8,128)S(1)}, u32[]{:S(2)}, u32[]{:S(2)}) async-start(f32[16,136,128]{2,1,0:T(8,128)} %inflow.1), calls=%async_computation.1 | async-start | bytes 2228224 | tf_op jit(solution)/shard_map/all_to_all | solution.py:396
  54.1 0.0 copy-done
  54.1 25.8 %near.2 = f32[4096,128]{1,0:T(8,128)} custom-call(s32[7,128]{1,0:T(8,128)} %near.3, s32[128]{0:T(128)} %count.1, f32[16,280,128]{2,1,0:T(8,128)} %copy-done, bf16[128,64,48]{2,1,0:T(8,128)(2,1)} %get-tuple-element.34.targets, bf16[128,64,128]{2,1,0:T(8,128)(2,1)} %get-tuple-element.35.vals_own, bf16[128,48,128]{2,1,0:T(8,128)(2,1)} %get-tuple-element.36.feats_own), custom_call_target="tpu_custom_call" | custom-call | flops 1000000000 | bytes 4194304 | tf_op jit(solution)/shard_map/near/pallas_call | solution.py:397
  79.9 0.0 all-to-all-done.1.recv
  79.9 0.0 copy-start.1
  79.9 1.0 %copy-done.1 = f32[16,136,128]{2,1,0:T(8,128)} copy-done((f32[16,136,128]{2,1,0:T(8,128)}, f32[16,136,128]{2,1,0:T(8,128)S(1)}, u32[]{:S(2)}) %copy-start.1) | copy-done | bytes 1114136
  80.9 11.4 %far.2 = f32[32,64,128]{2,1,0:T(8,128)} custom-call(s32[16,16]{1,0:T(8,128)} %far.3, f32[16,136,128]{2,1,0:T(8,128)} %copy-done.1, bf16[16,64,512]{2,1,0:T(8,128)(2,1)} %couple.1.cpl, f32[16,32,32]{2,1,0:T(8,128)} %get-tuple-element.31.gt_c, bf16[4096,128]{1,0:T(8,128)(2,1)} %get-tuple-element.32.wt, f32[4096,128]{1,0:T(8,128)} %near.2), custom_call_target="tpu_custom_call" | custom-call | flops 1000000000 | bytes 4194304 | tf_op jit(solution)/shard_map/far/pallas_call | solution.py:404
  (1 shorter events, 0.0 us)
Async XLA Ops:
  6.0 40.9 %all-to-all-start = ((f32[16,280,128]{2,1,0:T(8,128)}), f32[16,280,128]{2,1,0:T(8,128)S(1)}, u32[]{:S(2)}, u32[]{:S(2)}) async-start(f32[16,280,128]{2,1,0:T(8,128)} %get-tuple-element.21), calls=%async_computation | async-start | bytes 4587520 | tf_op jit(solution)/shard_map/all_to_all | solution.py:359
  23.5 10.1 %copy-start.2 = (f32[8,128]{1,0:T(8,128)S(1)}, f32[8,128]{1,0:T(8,128)}, u32[]{:S(2)}) copy-start(f32[8,128]{1,0:T(8,128)} %get-tuple-element.23) | copy-start | bytes 12292
  23.5 1.4 %collective-permute-start = (f32[1,8,128]{2,1,0:T(8,128)}, f32[1,8,128]{2,1,0:T(8,128)S(1)}, u32[]{:S(2)}, u32[]{:S(2)}) collective-permute-start(f32[1,8,128]{2,1,0:T(8,128)} %bitcast.8), channel_id=1, source_target_pairs={{0,16},{16,0},{32,48},{48,32},{64,80},{80,64},{96,112},{112,96},{1... | collective-permute-start | bytes 12296 | tf_op jit(solution)/shard_map/ppermute | solution.py:369
  25.6 8.1 %collective-permute-start.1 = (f32[2,8,128]{2,1,0:T(8,128)S(1)}, f32[2,8,128]{2,1,0:T(8,128)S(1)}, u32[]{:S(2)}, u32[]{:S(2)}) collective-permute-start(f32[2,8,128]{2,1,0:T(8,128)S(1)} %pad_maximum_fusion.2), channel_id=1, source_target_pairs={{0,32},{16,48},{32,0},{48,16},{64,96},{80,112},{96,64},{112,80},{1... | collective-permute-start | bytes 24584 | tf_op jit(solution)/shard_map/ppermute | solution.py:369
  33.6 10.2 %collective-permute-start.2 = (f32[4,8,128]{2,1,0:T(8,128)S(1)}, f32[4,8,128]{2,1,0:T(8,128)S(1)}, u32[]{:S(2)}, u32[]{:S(2)}) collective-permute-start(f32[4,8,128]{2,1,0:T(8,128)S(1)} %pad_maximum_fusion.1), channel_id=1, source_target_pairs={{0,64},{16,80},{32,96},{48,112},{64,0},{80,16},{96,32},{112,48},{1... | collective-permute-start | bytes 49160 | tf_op jit(solution)/shard_map/ppermute | solution.py:369
  46.8 7.2 %copy-start = (f32[16,280,128]{2,1,0:T(8,128)}, f32[16,280,128]{2,1,0:T(8,128)S(1)}, u32[]{:S(2)}) copy-start(f32[16,280,128]{2,1,0:T(8,128)S(1)} %all-to-all-done.recv) | copy-start | bytes 6881284
  46.9 33.1 %all-to-all-start.1 = ((f32[16,136,128]{2,1,0:T(8,128)}), f32[16,136,128]{2,1,0:T(8,128)S(1)}, u32[]{:S(2)}, u32[]{:S(2)}) async-start(f32[16,136,128]{2,1,0:T(8,128)} %inflow.1), calls=%async_computation.1 | async-start | bytes 2228224 | tf_op jit(solution)/shard_map/all_to_all | solution.py:396
  79.9 1.0 %copy-start.1 = (f32[16,136,128]{2,1,0:T(8,128)}, f32[16,136,128]{2,1,0:T(8,128)S(1)}, u32[]{:S(2)}) copy-start(f32[16,136,128]{2,1,0:T(8,128)S(1)} %all-to-all-done.1.recv) | copy-start | bytes 3342340
where the time goes:
time: 93 us; the launch traced here: 92.3 us
  Pallas kernels  68.8 us (74%)
  starting transfers between devices  19.8 us (21%)
  waiting for transfers between devices  1.38 us (1%)
  other arithmetic  1.3 us (1%)
  local copies, waits for them, and re-layouts  0.99 us (1%)
    pallas_call x1, Pallas kernels, body(): call(near_kernel, 'near', f32(4096, 128), [SMEM] * 2 + [VMEM] * 2 + [ANY]...  25.8 us
    pallas_call x1, Pallas kernels, body(): call(far_kernel, 'far', f32(32, 64, 128), [SMEM] + [VMEM] * 5, [pltpu.VME...  11.4 us
    pallas_call x1, Pallas kernels, body(): call(upward_kernel, 'upward', (b16(4096, 128), f32(128, 128), f32(8, 128)...  9.55 us
    all_to_all x1, starting transfers between devices, body(): recv = lax.all_to_all(payload, 'sub', 0, 0, tiled=True)  7.99 us
    all_to_all x1, starting transfers between devices, body(): far_recv = lax.all_to_all(far_payload, 'sub', 0, 0, tiled=True)  7.21 us
    pallas_call x1, Pallas kernels, body(): call(couple_kernel, 'couple', b16(16, 64, 512), [VMEM], [pltpu.VMEM((4, 5...  7.19 us
    pallas_call x1, Pallas kernels, body(): call(own_kernel, 'own', (b16(128, 64, 128), b16(128, 48, 128), b16(128, 6...  6.47 us
    pallas_call x1, Pallas kernels, body(): call(pack_kernel, 'pack', (f32(16, NEAR_ROWS, 128), f32(4096, 128), f32(1...  5.96 us
  transfers between devices with their start and end apart: 5, of which 1 were waited for; matrix products, arithmetic and copies ran while one was open for 1% of the time, Pallas kernels for 56%

commit v1 on v0

v1 whole, which is shorter than its diff:
```python
import math

import jax
import jax.numpy as jnp
from jax import lax
from jax.experimental import pallas as pl
from jax.experimental.pallas import tpu as pltpu
from jax.sharding import PartitionSpec as P

INV_FOUR_PI = 1.0 / (4.0 * math.pi)
EPS_SQ = 0.01
F32, BF16 = jnp.float32, jnp.bfloat16
NT = (((1,), (1,)), ((), ()))
NN = (((1,), (0,)), ((), ()))

POINTS_AT, NEAR_ROWS = 256, 280
INFLOW_AT, FAR_ROWS = 128, 136


def split(x):
    hi = x.astype(BF16)
    return hi, (x - hi.astype(F32)).astype(BF16)


def split3(x):
    hi = x.astype(BF16).astype(F32)
    rest = x - hi
    mid = rest.astype(BF16).astype(F32)
    return hi, mid, rest - mid


def mm(a, b, dims):
    return lax.dot_general(a, b, dims, preferred_element_type=F32)


def dot3(a, b, dims):
    ah, al = split(a)
    bh, bl = split(b)
    return mm(ah, bh, dims) + (mm(ah, bl, dims) + mm(al, bh, dims))


def low_half(shape):
    return lax.broadcasted_iota(jnp.int32, shape, len(shape) - 1) < 64


def rows(i, n):
    return pl.ds(pl.multiple_of(i * n, n), n)


def twice(block):
    return jnp.transpose(jnp.concatenate([block, block], 0))


def pack_kernel(send, src, crd, out, src_out, pts_out, src_t, pts_t, planes, blocks, sems):
    def source_rows(i, _):
        for r in range(8):
            planes[i * 8 + r] = twice(src[i * 8 + r])
        return 0

    lax.fori_loop(0, 4, source_rows, 0)

    def eight_leaves(g, _):
        block = jnp.transpose(planes[:, rows(g, 8), :], (1, 0, 2))
        src_t[rows(g, 256), :] = block.reshape(256, 128)
        return 0

    lax.fori_loop(0, 16, eight_leaves, 0)
    for c in range(3):
        planes[c] = twice(crd[c] - 1.0)
    for c in range(3, 8):
        planes[c] = jnp.zeros((128, 128), F32)

    def eight_points(g, _):
        block = jnp.transpose(planes[0:8, rows(g, 8), :], (1, 0, 2))
        pts_t[rows(g, 64), :] = block.reshape(64, 128)
        return 0

    lax.fori_loop(0, 16, eight_points, 0)
    copies = [pltpu.make_async_copy(src_t, src_out, sems.at[16]), pltpu.make_async_copy(pts_t, pts_out, sems.at[17])]
    for copy in copies:
        copy.start()
    low = low_half((32, 128))
    low8 = low_half((8, 128))

    def block_copy(q):
        return pltpu.make_async_copy(blocks.at[q], out.at[q], sems.at[q])

    def one_peer(q, _):
        for p in range(8):
            first, second = send[q, 2 * p], send[q, 2 * p + 1]
            blocks[q, pl.ds(32 * p, 32), :] = jnp.where(low, src_t[rows(first, 32), :], src_t[rows(second, 32), :])
            pts = jnp.where(low8, pts_t[rows(first, 8), :], pts_t[rows(second, 8), :])
            blocks[q, pl.ds(POINTS_AT + 3 * p, 3), :] = pts[:3]
        block_copy(q).start()
        return 0

    lax.fori_loop(0, 16, one_peer, 0)
    for copy in copies + [block_copy(q) for q in range(16)]:
        copy.wait()


def upward_kernel(src_t, bas, tra, gt, wt, skel, own, gt_4, planes, w_t, gt_c):
    gt_c[...] = jnp.transpose(gt[...], (1, 0, 2))
    for i in range(4):
        gt_4[i] = jnp.concatenate([gt_c[4 * i + u] for u in range(4)], 1)

    def w_rows(jb, _):
        acc = [jnp.zeros((64, 128), F32) for _ in range(2)]
        for k in range(32):
            block = bas[k]
            for i in range(2):
                acc[i] = acc[i] + tra[jb * 2 + i, k : k + 1, :] * block
        for i in range(2):
            planes[jb * 2 + i] = twice(acc[i])
        return 0

    lax.fori_loop(0, 16, w_rows, 0)
    low = low_half((256, 128))

    def eight_leaves(g, _):
        block = jnp.transpose(planes[:, rows(g, 8), :], (1, 0, 2)).reshape(256, 128)
        w_t[rows(g, 256), :] = block
        hi = block.astype(BF16).astype(F32)
        wt[rows(g, 256), :] = jnp.where(low, hi, block - hi).astype(BF16)
        return 0

    lax.fori_loop(0, 16, eight_leaves, 0)
    low32 = low_half((32, 128))

    def one_parent(c):
        ws, ss = [], []
        for pair in range(4):
            first, second = [rows(c * 8 + pair * 2 + i, 32) for i in (0, 1)]
            w = jnp.where(low32, w_t[first, :], w_t[second, :])
            s = jnp.where(low32, src_t[first, :], src_t[second, :])
            ws.append(jnp.concatenate(split(w), 0))
            ss.append(jnp.concatenate(split(s), 0))
        total = mm(jnp.concatenate(ws, 1), jnp.concatenate(ss, 1), NT)
        both = total[:32] + total[32:]
        return both[:, :32] + both[:, 32:]

    def four_parents(cg, total):
        blocks = [one_parent(cg * 4 + i) for i in range(4)]
        skel[rows(cg, 32), :] = jnp.concatenate(blocks, 1)
        for i in range(4):
            total = total + dot3(gt_c[cg * 4 + i], blocks[i], NN)
        return total

    total = lax.fori_loop(0, 4, four_parents, jnp.zeros((32, 32), F32))
    own[...] = jnp.concatenate([total[8 * i : 8 * i + 8] for i in range(4)], 1)


def unpack(packed):
    return jnp.concatenate([packed[:, 32 * i : 32 * i + 32] for i in range(4)], 0)


def inflow_kernel(group, row, parts, skel, out):
    total = jnp.zeros((32, 32), F32)
    for m in range(1, 8):
        h = group[0] ^ m
        total = total + dot3(row[:, pl.ds(h, 1), :].reshape(32, 32), unpack(parts[m]), NN)
    packed = jnp.concatenate([total[8 * i : 8 * i + 8] for i in range(4)], 1)
    for q in range(16):
        out[q, 0:128, :] = skel[...]
        out[q, 128:136, :] = packed


def couple_kernel(cpl, lines):
    def some_rows(i, _):
        for u in range(2):
            k = i * 2 + u
            for fg in range(4):
                lines[fg, pl.ds(k, 16, stride=32), :] = jnp.concatenate([cpl[k, 4 * fg + v] for v in range(4)], 1)
        return 0

    lax.fori_loop(0, 16, some_rows, 0)


def point_rows(x, target):
    line = lax.broadcasted_iota(jnp.int32, x.shape, 0)
    norm = jnp.sum(jnp.where(line < 3, x * x, 0.0), axis=0, keepdims=True)
    if target:
        return jnp.where(line < 3, -2.0 * x, jnp.where(line == 3, 1.0, jnp.where(line == 4, norm + EPS_SQ, 0.0)))
    return jnp.where(line < 3, x, jnp.where(line == 3, norm, jnp.where(line == 4, 1.0, 0.0)))


def own_kernel(pts_t, feats, targets):
    def some_leaves(i, _):
        for u in range(8):
            l = i * 8 + u
            x = pts_t[rows(l, 8), :]
            feats[rows(l, 8), :] = point_rows(x, False)
            a, b, c = split3(point_rows(x, True))
            targets[l] = jnp.transpose(jnp.concatenate([a, a, b, a, b, c], 0))[:64].astype(BF16)
        return 0

    lax.fori_loop(0, 16, some_leaves, 0)


def near_kernel(near, count, recv, targets, vals_own, feats_own, out, vals, feats, total, planes, ring_a, ring_b, sems):
    copies = [
        pltpu.make_async_copy(vals_own, vals.at[pl.ds(0, 4096), :], sems.at[0]),
        pltpu.make_async_copy(feats_own, feats.at[pl.ds(0, 1024), :], sems.at[1]),
    ]
    for copy in copies:
        copy.start()
    low = low_half((32, 128))
    low8 = low_half((8, 128))
    vals[pl.ds(384 * 32, 32), :] = jnp.zeros((32, 128), F32)
    feats[pl.ds(384 * 8, 8), :] = point_rows(jnp.zeros((8, 128), F32), False)

    def one_sender(s, _):
        for p in range(8):
            slot = 128 + s * 16 + 2 * p
            x = recv[s, pl.ds(32 * p, 32), :]
            y = pltpu.roll(x, 64, 1)
            vals[rows(slot, 32), :] = jnp.where(low, x, y)
            vals[rows(slot + 1, 32), :] = jnp.where(low, y, x)
            x = recv[s, pl.ds(POINTS_AT + 3 * p, 3), :]
            x = point_rows(jnp.concatenate([x, jnp.zeros((5, 128), F32)], 0), False)
            y = pltpu.roll(x, 64, 1)
            feats[rows(slot, 8), :] = jnp.where(low8, x, y)
            feats[rows(slot + 1, 8), :] = jnp.where(low8, y, x)
        return 0

    lax.fori_loop(0, 16, one_sender, 0)
    for copy in copies:
        copy.wait()

    def pairs_of(l):
        live = count[l]
        slots = [jnp.where(e < live, near[e, l], 384) if e < 7 else 384 for e in range(8)]
        return [(slots[2 * i], slots[2 * i + 1]) for i in range(4)]

    def evaluate(group, ring):
        for u in range(UNROLL):
            l = group * UNROLL + u
            x = [jnp.where(low8, feats[rows(a, 8), :], feats[rows(b, 8), :]) for a, b in pairs_of(l)]
            a, b, c = split3(jnp.concatenate(x, 1))
            points = jnp.concatenate([a, b, a, c, b, a], 0).astype(BF16)
            ring[u] = lax.rsqrt(mm(targets[l], points, NN))

    def multiply(group, ring):
        for u in range(UNROLL):
            l = group * UNROLL + u
            x = [jnp.where(low, vals[rows(a, 32), :], vals[rows(b, 32), :]) for a, b in pairs_of(l)]
            values = jnp.concatenate(split(jnp.concatenate(x, 1)), 0)
            acc = mm(values, jnp.concatenate(split(ring[u]), 0), NT)
            total[rows(l, 32), :] = (acc[:32] + acc[32:]) * INV_FOUR_PI

    groups = 128 // UNROLL
    evaluate(0, ring_a)

    def two_groups(i, _):
        evaluate(2 * i + 1, ring_b)
        multiply(2 * i, ring_a)
        evaluate(jnp.minimum(2 * i + 2, groups - 1), ring_a)
        multiply(2 * i + 1, ring_b)
        return 0

    lax.fori_loop(0, groups // 2, two_groups, 0)

    def eight_leaves(g, _):
        block = total[rows(g, 256), :].reshape(8, 32, 128)
        planes[:, rows(g, 8), :] = jnp.transpose(block, (1, 0, 2))
        return 0

    lax.fori_loop(0, 16, eight_leaves, 0)

    def some_rhs(i, _):
        for u in range(8):
            x = jnp.transpose(planes[i * 8 + u])
            out[i * 8 + u] = x[:64] + x[64:]
        return 0

    lax.fori_loop(0, 4, some_rhs, 0)


UNROLL = 4


def far_kernel(far, recv, cpl, gt_4, wt, near, out, sums, planes):
    lane_group = lax.broadcasted_iota(jnp.int32, (32, 128), 1) // 32

    def one_parent(c):
        blocks = []
        for f in range(16):
            q = far[f, c]
            tile = recv[q >> 4, rows((q >> 2) & 3, 32), :]
            blocks.append(jnp.concatenate(split(jnp.where(lane_group == (q & 3), tile, 0.0)), 1))
        left = jnp.concatenate(split(jnp.concatenate([cpl[i, rows(c, 32), :] for i in range(4)], 1)), 0)
        acc = mm(left, jnp.concatenate(blocks, 0), NN)
        both = acc[:32] + acc[32:]
        x = both[:, :128] + both[:, 128:]
        x = x + pltpu.roll(x, 64, 1)
        sums[rows(c, 32), :] = x + pltpu.roll(x, 32, 1)

    def some_parents(i, _):
        for u in range(4):
            one_parent(i * 4 + u)
        return 0

    lax.fori_loop(0, 4, some_parents, 0)
    packed = recv[0, pl.ds(INFLOW_AT, 8), :]
    for s in range(1, 16):
        packed = packed + recv[s, pl.ds(INFLOW_AT, 8), :]
    inflow_t = jnp.transpose(jnp.pad(unpack(packed), ((0, 96), (0, 96))))[:32, :32]

    def four_parents(i, _):
        x = jnp.transpose(sums[rows(i, 128), :])[:32] + dot3(inflow_t, gt_4[i], NN)
        field = jnp.concatenate(split(x), 0)
        for u in range(4):
            leaves = []
            for v in range(8):
                acc = mm(field[:, 32 * u : 32 * u + 32], wt[rows(i * 32 + u * 8 + v, 32), :], NN)
                leaves.append(acc[:32] + acc[32:])
            planes[:, rows(i * 4 + u, 8), :] = jnp.transpose(jnp.stack(leaves, 0), (1, 0, 2))
        return 0

    lax.fori_loop(0, 4, four_parents, 0)

    def some_rhs(i, _):
        for u in range(8):
            x = jnp.transpose(planes[i * 8 + u])
            out[i * 8 + u] = x[:64] + x[64:] + near[i * 8 + u]
        return 0

    lax.fori_loop(0, 4, some_rhs, 0)


VMEM = pl.BlockSpec(memory_space=pltpu.VMEM)
SMEM = pl.BlockSpec(memory_space=pltpu.SMEM)
ANY = pl.BlockSpec(memory_space=pl.ANY)


def f32(*shape):
    return jax.ShapeDtypeStruct(shape, F32)


def b16(*shape):
    return jax.ShapeDtypeStruct(shape, BF16)


def call(kernel, name, out_shape, in_specs, scratch=(), mib=56, out_specs=None):
    several = isinstance(out_shape, tuple)
    return pl.pallas_call(
        kernel,
        out_shape=out_shape,
        in_specs=in_specs,
        out_specs=out_specs or ((VMEM,) * len(out_shape) if several else VMEM),
        scratch_shapes=scratch,
        compiler_params=pltpu.CompilerParams(vmem_limit_bytes=mib << 20),
        cost_estimate=pl.CostEstimate(flops=10**9, bytes_accessed=4 << 20, transcendentals=0),
        name=name,
    )


def body(
    sources,
    coords,
    leaf_basis,
    transfer,
    send_list,
    near_list,
    near_count,
    far_list,
    coupling,
    group_transfer,
    group_coupling,
):
    planes = pltpu.VMEM((32, 128, 128), F32)
    payload, src_t, pts_t = call(
        pack_kernel,
        "pack",
        (f32(16, NEAR_ROWS, 128), f32(4096, 128), f32(1024, 128)),
        [SMEM, VMEM, VMEM],
        [
            pltpu.VMEM((4096, 128), F32),
            pltpu.VMEM((1024, 128), F32),
            planes,
            pltpu.VMEM((16, NEAR_ROWS, 128), F32),
            pltpu.SemaphoreType.DMA((18,)),
        ],
        out_specs=(ANY,) * 3,
    )(send_list, sources, coords)
    recv = lax.all_to_all(payload, "sub", 0, 0, tiled=True)
    wt, skel, own, gt_4 = call(
        upward_kernel,
        "upward",
        (b16(4096, 128), f32(128, 128), f32(8, 128), f32(4, 32, 128)),
        [VMEM] * 4,
        [planes, pltpu.VMEM((4096, 128), F32), pltpu.VMEM((16, 32, 32), F32)],
    )(src_t, leaf_basis, transfer, jnp.transpose(group_transfer, (0, 2, 1)))
    parts = own[None]
    for step in (1, 2, 4):
        other = lax.ppermute(parts, "grp", [(i, i ^ step) for i in range(8)])
        parts = jnp.concatenate([parts, other], 0)
    group = lax.axis_index("grp").astype(jnp.int32).reshape(1)
    far_payload = pl.pallas_call(
        inflow_kernel,
        out_shape=f32(16, FAR_ROWS, 128),
        grid_spec=pltpu.PrefetchScalarGridSpec(
            num_scalar_prefetch=1,
            grid=(1,),
            in_specs=[
                pl.BlockSpec((32, pl.Squeezed(), 8, 32), lambda i, g: (0, g[0], 0, 0)),
                pl.BlockSpec((8, 8, 128), lambda i, g: (0, 0, 0)),
                pl.BlockSpec((128, 128), lambda i, g: (0, 0)),
            ],
            out_specs=pl.BlockSpec((16, FAR_ROWS, 128), lambda i, g: (0, 0, 0)),
        ),
        name="inflow",
    )(group, jnp.transpose(group_coupling, (0, 2, 3, 1)), parts, skel)
    cpl = call(couple_kernel, "couple", f32(4, 512, 128), [VMEM])(jnp.transpose(coupling, (0, 2, 3, 1)))
    feats, targets = call(own_kernel, "own", (f32(1024, 128), b16(128, 64, 48)), [VMEM])(pts_t)
    recv, far_payload, cpl, feats, targets = lax.optimization_barrier((recv, far_payload, cpl, feats, targets))
    far_recv = lax.all_to_all(far_payload, "sub", 0, 0, tiled=True)
    near = call(
        near_kernel,
        "near",
        f32(32, 64, 128),
        [SMEM] * 2 + [VMEM] * 2 + [ANY] * 2,
        [
            pltpu.VMEM((385 * 32, 128), F32),
            pltpu.VMEM((385 * 8, 128), F32),
            pltpu.VMEM((4096, 128), F32),
            planes,
            pltpu.VMEM((UNROLL, 64, 512), F32),
            pltpu.VMEM((UNROLL, 64, 512), F32),
            pltpu.SemaphoreType.DMA((2,)),
        ],
    )(near_list, near_count, recv, targets, src_t, feats)
    return call(
        far_kernel,
        "far",
        f32(32, 64, 128),
        [SMEM] + [VMEM] * 5,
        [pltpu.VMEM((512, 128), F32), planes],
    )(far_list, far_recv, cpl, gt_4, wt, near)


def solution(mesh):
    leaves = P(None, None, ("grp", "sub"))
    return jax.shard_map(
        body,
        mesh=mesh,
        in_specs=(
            leaves,
            leaves,
            leaves,
            leaves,
            P(("grp", "sub"), None),
            P(None, ("grp", "sub")),
            P(("grp", "sub")),
            P(None, ("grp", "sub")),
            P(None, None, None, ("grp", "sub")),
            leaves,
            P(),
        ),
        out_specs=leaves,
        check_vma=False,
    )
```

time: 93 us -> 77.8 us (0.84)
  Pallas kernels: 68.8 us -> 53.2 us
  waiting for transfers between devices: 1.38 us -> 5.46 us
  starting transfers between devices: 19.8 us -> 16.3 us
    pallas_call x3, Pallas kernels: 39.5 us -> 27.7 us  [the longest x1 17.6 us: body(): call(near_kernel, 'near', f32(32, 64, 128), [SMEM] * 2 + [VMEM] * 2 + [AN...]
    all_to_all x1, starting transfers between devices: 7.21 us -> 3.77 us  [body(): far_recv = lax.all_to_all(far_payload, 'sub', 0, 0, tiled=True)]
    all_to_all x1, waiting for transfers between devices: 0.01 us -> 3.44 us  [body(): recv = lax.all_to_all(payload, 'sub', 0, 0, tiled=True)]
    pallas_call x1, Pallas kernels: 11.4 us -> 8.14 us  [body(): call(far_kernel, 'far', f32(32, 64, 128), [SMEM] + [VMEM] * 5, [pltpu.VME...]
  transfers between devices with their start and end apart: 5 -> 5, of which waited for: 1 -> 3; matrix products, arithmetic and copies ran while one was open for 1% -> 2% of each run, Pallas kernels for 56% -> 51%
where the time goes in v1:
time: 77.8 us; the launch traced here: 77.4 us
  Pallas kernels  53.2 us (68%)
  starting transfers between devices  16.3 us (21%)
  waiting for transfers between devices  5.46 us (7%)
  other arithmetic  1.3 us (2%)
  local copies, waits for them, and re-layouts  1 us (1%)
    pallas_call x1, Pallas kernels, body(): call(near_kernel, 'near', f32(32, 64, 128), [SMEM] * 2 + [VMEM] * 2 + [AN...  17.6 us
    pallas_call x1, Pallas kernels, body(): call(upward_kernel, 'upward', (b16(4096, 128), f32(128, 128), f32(8, 128)...  9.65 us
    pallas_call x1, Pallas kernels, body(): call(far_kernel, 'far', f32(32, 64, 128), [SMEM] + [VMEM] * 5, [pltpu.VME...  8.14 us
    all_to_all x1, starting transfers between devices, body(): recv = lax.all_to_all(payload, 'sub', 0, 0, tiled=True)  8 us
    pallas_call x1, Pallas kernels, body(): call(couple_kernel, 'couple', f32(4, 512, 128), [VMEM])  5.78 us
    pallas_call x1, Pallas kernels, body(): call(pack_kernel, 'pack', (f32(16, NEAR_ROWS, 128), f32(4096, 128), f32(1...  5.31 us
    ppermute x3, starting transfers between devices, body(): other = lax.ppermute(parts, 'grp', [(i, i ^ step) for i in range(8)])  4.56 us
    pallas_call x1, Pallas kernels, body(): call(own_kernel, 'own', (f32(1024, 128), b16(128, 64, 48)), [VMEM])(pts_t)  4.34 us
  transfers between devices with their start and end apart: 5, of which 3 were waited for; matrix products, arithmetic and copies ran while one was open for 2% of the time, Pallas kernels for 51%

profile of v1, /device:TPU:0, one launch (start us, length us, event | category | flops | bytes accessed | tf_op | source)
XLA Modules:
  0.0 77.4 jit_solution(16329070841690039942)
XLA Ops:
  0.0 5.3 %pack.1 = (f32[16,280,128]{2,1,0:T(8,128)}, f32[4096,128]{1,0:T(8,128)}, f32[1024,128]{1,0:T(8,128)}) custom-call(s32[16,16]{1,0:T(8,128)} %send.1, f32[32,64,128]{2,1,0:T(8,128)} %src.1, f32[3,64,128]{2,1,0:T(8,128)} %crd.1), custom_call_target="tpu_custom_call" | custom-call | flops 1000000000 | bytes 4194304 | tf_op jit(solution)/shard_map/pack/pallas_call | solution.py:372
  5.3 8.0 %all-to-all-start = ((f32[16,280,128]{2,1,0:T(8,128)}), f32[16,280,128]{2,1,0:T(8,128)S(1)}, u32[]{:S(2)}, u32[]{:S(2)}) async-start(f32[16,280,128]{2,1,0:T(8,128)} %get-tuple-element.19), calls=%async_computation | async-start | bytes 4587520 | tf_op jit(solution)/shard_map/all_to_all | solution.py:386
  13.3 9.7 %upward.1 = (bf16[4096,128]{1,0:T(8,128)(2,1)}, f32[128,128]{1,0:T(8,128)}, f32[8,128]{1,0:T(8,128)}, f32[4,32,128]{2,1,0:T(8,128)}) custom-call(f32[4096,128]{1,0:T(8,128)} %get-tuple-element.20.src_t.vals_own, f32[32,64,128]{2,1,0:T(8,128)} %bas.1, f32[32,32,128]{2,1,0:T(8,128)} %tra.1, f32[32,16,32]{2,1,0:T(8,128)} %bitcast.7), custom_call_target="tpu_custom_call" | custom-call | flops 1000000000 | bytes 4194304 | tf_op jit(solution)/shard_map/upward/pallas_call | solution.py:387
  23.0 0.0 collective-permute-start
  23.0 1.4 %collective-permute-done = f32[1,8,128]{2,1,0:T(8,128)S(1)} collective-permute-done((f32[1,8,128]{2,1,0:T(8,128)}, f32[1,8,128]{2,1,0:T(8,128)S(1)}, u32[]{:S(2)}, u32[]{:S(2)}) %collective-permute-start) | collective-permute-done | bytes 4128 | tf_op jit(solution)/shard_map/ppermute | solution.py:396
  24.4 0.7 pad_maximum_fusion.2
  25.0 1.6 %collective-permute-start.1 = (f32[2,8,128]{2,1,0:T(8,128)S(1)}, f32[2,8,128]{2,1,0:T(8,128)S(1)}, u32[]{:S(2)}, u32[]{:S(2)}) collective-permute-start(f32[2,8,128]{2,1,0:T(8,128)S(1)} %pad_maximum_fusion.2), channel_id=1, source_target_pairs={{0,32},{16,48},{32,0},{48,16},{64,96},{80,112},{96,64},{112,80},{1... | collective-permute-start | bytes 24584 | tf_op jit(solution)/shard_map/ppermute | solution.py:396
  26.6 0.0 copy-start.2
  26.6 5.8 %couple.1.cpl = f32[4,512,128]{2,1,0:T(8,128)} custom-call(f32[32,16,16,32]{3,2,1,0:T(8,128)} %bitcast.5), custom_call_target="tpu_custom_call" | custom-call | flops 1000000000 | bytes 4194304 | tf_op jit(solution)/shard_map/couple/pallas_call | solution.py:414
  32.4 0.0 collective-permute-done.1
  32.4 0.0 copy-done.2
  32.4 3.0 %collective-permute-start.2 = (f32[4,8,128]{2,1,0:T(8,128)S(1)}, f32[4,8,128]{2,1,0:T(8,128)S(1)}, u32[]{:S(2)}, u32[]{:S(2)}) collective-permute-start(f32[4,8,128]{2,1,0:T(8,128)S(1)} %pad_maximum_fusion.1), channel_id=1, source_target_pairs={{0,64},{16,80},{32,96},{48,112},{64,0},{80,16},{96,32},{112,48},{1... | collective-permute-start | bytes 49160 | tf_op jit(solution)/shard_map/ppermute | solution.py:396
  35.4 4.3 %own.1 = (f32[1024,128]{1,0:T(8,128)}, bf16[128,64,48]{2,1,0:T(8,128)(2,1)}) custom-call(f32[1024,128]{1,0:T(8,128)} %get-tuple-element.23.pts_t), custom_call_target="tpu_custom_call" | custom-call | flops 1000000000 | bytes 4194304 | tf_op jit(solution)/shard_map/own/pallas_call | solution.py:415
  39.7 0.0 collective-permute-done.2
  39.7 0.6 pad_maximum_fusion.parts
  40.4 2.4 %inflow.1 = f32[16,136,128]{2,1,0:T(8,128)} custom-call(s32[1]{0:T(128)} %bitcast.group, f32[32,8,8,32]{3,2,1,0:T(8,128)} %bitcast.6, f32[8,8,128]{2,1,0:T(8,128)} %pad_maximum_fusion.parts, f32[128,128]{1,0:T(8,128)} %get-tuple-element.22.skel), custom_call_target="tpu_custom_call" | custom-call | tf_op jit(solution)/shard_map/inflow/pallas_call | solution.py:399
  42.8 3.4 %all-to-all-done.recv = f32[16,280,128]{2,1,0:T(8,128)S(1)} async-done(((f32[16,280,128]{2,1,0:T(8,128)}), f32[16,280,128]{2,1,0:T(8,128)S(1)}, u32[]{:S(2)}, u32[]{:S(2)}) %all-to-all-start) | async-done | bytes 2293792 | tf_op jit(solution)/shard_map/all_to_all | solution.py:386
  46.2 0.0 copy-start
  46.2 3.8 %all-to-all-start.1 = ((f32[16,136,128]{2,1,0:T(8,128)}), f32[16,136,128]{2,1,0:T(8,128)S(1)}, u32[]{:S(2)}, u32[]{:S(2)}) async-start(f32[16,136,128]{2,1,0:T(8,128)} %inflow.1), calls=%async_computation.1 | async-start | bytes 2228224 | tf_op jit(solution)/shard_map/all_to_all | solution.py:417
  50.0 0.0 copy-done
  50.0 17.6 %near.2 = f32[32,64,128]{2,1,0:T(8,128)} custom-call(s32[7,128]{1,0:T(8,128)} %near.3, s32[128]{0:T(128)} %count.1, f32[16,280,128]{2,1,0:T(8,128)} %copy-done, bf16[128,64,48]{2,1,0:T(8,128)(2,1)} %get-tuple-element.31.targets, f32[4096,128]{1,0:T(8,128)} %get-tuple-element.20.src_t.vals_own, f32[1024,128]{1,0:T(8,128)} %get-tuple-element.32.feats_own), custom_call_target="tpu_custom_call" | custom-call | flops 1000000000 | bytes 4194304 | tf_op jit(solution)/shard_map/near/pallas_call | solution.py:418
  67.6 0.6 all-to-all-done.1.recv
  68.2 0.0 copy-start.1
  68.2 1.0 %copy-done.1 = f32[16,136,128]{2,1,0:T(8,128)} copy-done((f32[16,136,128]{2,1,0:T(8,128)}, f32[16,136,128]{2,1,0:T(8,128)S(1)}, u32[]{:S(2)}) %copy-start.1) | copy-done | bytes 1114136
  69.2 8.1 %far.2 = f32[32,64,128]{2,1,0:T(8,128)} custom-call(s32[16,16]{1,0:T(8,128)} %far.3, f32[16,136,128]{2,1,0:T(8,128)} %copy-done.1, f32[4,512,128]{2,1,0:T(8,128)} %couple.1.cpl, f32[4,32,128]{2,1,0:T(8,128)} %get-tuple-element.28.gt_4, bf16[4096,128]{1,0:T(8,128)(2,1)} %get-tuple-element.29.wt, f32[32,64,128]{2,1,0:T(8,128)} %near.2), custom_call_target="tpu_custom_call" | custom-call | flops 1000000000 | bytes 4194304 | tf_op jit(solution)/shard_map/far/pallas_call | solution.py:433
  (1 shorter events, 0.0 us)
Async XLA Ops:
  5.3 40.9 %all-to-all-start = ((f32[16,280,128]{2,1,0:T(8,128)}), f32[16,280,128]{2,1,0:T(8,128)S(1)}, u32[]{:S(2)}, u32[]{:S(2)}) async-start(f32[16,280,128]{2,1,0:T(8,128)} %get-tuple-element.19), calls=%async_computation | async-start | bytes 4587520 | tf_op jit(solution)/shard_map/all_to_all | solution.py:386
  23.0 1.4 %collective-permute-start = (f32[1,8,128]{2,1,0:T(8,128)}, f32[1,8,128]{2,1,0:T(8,128)S(1)}, u32[]{:S(2)}, u32[]{:S(2)}) collective-permute-start(f32[1,8,128]{2,1,0:T(8,128)} %bitcast.8), channel_id=1, source_target_pairs={{0,16},{16,0},{32,48},{48,32},{64,80},{80,64},{96,112},{112,96},{1... | collective-permute-start | bytes 12296 | tf_op jit(solution)/shard_map/ppermute | solution.py:396
  25.0 7.4 %collective-permute-start.1 = (f32[2,8,128]{2,1,0:T(8,128)S(1)}, f32[2,8,128]{2,1,0:T(8,128)S(1)}, u32[]{:S(2)}, u32[]{:S(2)}) collective-permute-start(f32[2,8,128]{2,1,0:T(8,128)S(1)} %pad_maximum_fusion.2), channel_id=1, source_target_pairs={{0,32},{16,48},{32,0},{48,16},{64,96},{80,112},{96,64},{112,80},{1... | collective-permute-start | bytes 24584 | tf_op jit(solution)/shard_map/ppermute | solution.py:396
  26.6 5.8 %copy-start.2 = (f32[8,128]{1,0:T(8,128)S(1)}, f32[8,128]{1,0:T(8,128)}, u32[]{:S(2)}) copy-start(f32[8,128]{1,0:T(8,128)} %get-tuple-element.21) | copy-start | bytes 12292
  32.4 7.3 %collective-permute-start.2 = (f32[4,8,128]{2,1,0:T(8,128)S(1)}, f32[4,8,128]{2,1,0:T(8,128)S(1)}, u32[]{:S(2)}, u32[]{:S(2)}) collective-permute-start(f32[4,8,128]{2,1,0:T(8,128)S(1)} %pad_maximum_fusion.1), channel_id=1, source_target_pairs={{0,64},{16,80},{32,96},{48,112},{64,0},{80,16},{96,32},{112,48},{1... | collective-permute-start | bytes 49160 | tf_op jit(solution)/shard_map/ppermute | solution.py:396
  46.2 3.8 %copy-start = (f32[16,280,128]{2,1,0:T(8,128)}, f32[16,280,128]{2,1,0:T(8,128)S(1)}, u32[]{:S(2)}) copy-start(f32[16,280,128]{2,1,0:T(8,128)S(1)} %all-to-all-done.recv) | copy-start | bytes 6881284
  46.2 22.0 %all-to-all-start.1 = ((f32[16,136,128]{2,1,0:T(8,128)}), f32[16,136,128]{2,1,0:T(8,128)S(1)}, u32[]{:S(2)}, u32[]{:S(2)}) async-start(f32[16,136,128]{2,1,0:T(8,128)} %inflow.1), calls=%async_computation.1 | async-start | bytes 2228224 | tf_op jit(solution)/shard_map/all_to_all | solution.py:417
  68.2 1.0 %copy-start.1 = (f32[16,136,128]{2,1,0:T(8,128)}, f32[16,136,128]{2,1,0:T(8,128)S(1)}, u32[]{:S(2)}) copy-start(f32[16,136,128]{2,1,0:T(8,128)S(1)} %all-to-all-done.1.recv) | copy-start | bytes 3342340

commit v2 on v1

--- a/solution.py
+++ b/solution.py
@@ -51,7 +51,7 @@
     return jnp.transpose(jnp.concatenate([block, block], 0))
 
 
-def pack_kernel(send, src, crd, out, src_out, pts_out, src_t, pts_t, planes, blocks, sems):
+def pack_kernel(send, crd, src, out, src_out, pts_out, src_t, pts_t, planes, blocks, sems):
     def source_rows(i, _):
         for r in range(8):
             planes[i * 8 + r] = twice(src[i * 8 + r])
@@ -59,23 +59,26 @@
 
     lax.fori_loop(0, 4, source_rows, 0)
 
-    def eight_leaves(g, _):
-        block = jnp.transpose(planes[:, rows(g, 8), :], (1, 0, 2))
-        src_t[rows(g, 256), :] = block.reshape(256, 128)
-        return 0
-
-    lax.fori_loop(0, 16, eight_leaves, 0)
+    def eight_leaves(i, _):
+        for g in (2 * i, 2 * i + 1):
+            block = jnp.transpose(planes[:, rows(g, 8), :], (1, 0, 2))
+            src_t[rows(g, 256), :] = block.reshape(256, 128)
+        return 0
+
+    lax.fori_loop(0, 8, eight_leaves, 0)
     for c in range(3):
         planes[c] = twice(crd[c] - 1.0)
     for c in range(3, 8):
         planes[c] = jnp.zeros((128, 128), F32)
 
-    def eight_points(g, _):
-        block = jnp.transpose(planes[0:8, rows(g, 8), :], (1, 0, 2))
-        pts_t[rows(g, 64), :] = block.reshape(64, 128)
-        return 0
-
-    lax.fori_loop(0, 16, eight_points, 0)
+    def eight_points(i, _):
+        for u in range(4):
+            g = i * 4 + u
+            block = jnp.transpose(planes[0:8, rows(g, 8), :], (1, 0, 2))
+            pts_t[rows(g, 64), :] = block.reshape(64, 128)
+        return 0
+
+    lax.fori_loop(0, 4, eight_points, 0)
     copies = [pltpu.make_async_copy(src_t, src_out, sems.at[16]), pltpu.make_async_copy(pts_t, pts_out, sems.at[17])]
     for copy in copies:
         copy.start()
@@ -85,16 +88,17 @@
     def block_copy(q):
         return pltpu.make_async_copy(blocks.at[q], out.at[q], sems.at[q])
 
-    def one_peer(q, _):
-        for p in range(8):
-            first, second = send[q, 2 * p], send[q, 2 * p + 1]
-            blocks[q, pl.ds(32 * p, 32), :] = jnp.where(low, src_t[rows(first, 32), :], src_t[rows(second, 32), :])
-            pts = jnp.where(low8, pts_t[rows(first, 8), :], pts_t[rows(second, 8), :])
-            blocks[q, pl.ds(POINTS_AT + 3 * p, 3), :] = pts[:3]
-        block_copy(q).start()
-        return 0
-
-    lax.fori_loop(0, 16, one_peer, 0)
+    def two_peers(i, _):
+        for q in (2 * i, 2 * i + 1):
+            for p in range(8):
+                first, second = send[q, 2 * p], send[q, 2 * p + 1]
+                blocks[q, pl.ds(32 * p, 32), :] = jnp.where(low, src_t[rows(first, 32), :], src_t[rows(second, 32), :])
+                pts = jnp.where(low8, pts_t[rows(first, 8), :], pts_t[rows(second, 8), :])
+                blocks[q, pl.ds(POINTS_AT + 3 * p, 3), :] = pts[:3]
+            block_copy(q).start()
+        return 0
+
+    lax.fori_loop(0, 8, two_peers, 0)
     for copy in copies + [block_copy(q) for q in range(16)]:
         copy.wait()
 
@@ -197,8 +201,11 @@
     lax.fori_loop(0, 16, some_leaves, 0)
 
 
-def near_kernel(near, count, recv, targets, vals_own, feats_own, out, vals, feats, total, planes, ring_a, ring_b, sems):
+def near_kernel(
+    near, count, recv, targets_in, vals_own, feats_own, out, vals, feats, targets, total, planes, result, ring_a, ring_b, sems
+):
     copies = [
+        pltpu.make_async_copy(targets_in, targets, sems.at[2]),
         pltpu.make_async_copy(vals_own, vals.at[pl.ds(0, 4096), :], sems.at[0]),
         pltpu.make_async_copy(feats_own, feats.at[pl.ds(0, 1024), :], sems.at[1]),
     ]
@@ -267,19 +274,31 @@
 
     lax.fori_loop(0, 16, eight_leaves, 0)
 
+    def out_copy(i):
+        return pltpu.make_async_copy(result.at[pl.ds(i * 8, 8)], out.at[pl.ds(i * 8, 8)], sems.at[3 + i])
+
     def some_rhs(i, _):
         for u in range(8):
             x = jnp.transpose(planes[i * 8 + u])
-            out[i * 8 + u] = x[:64] + x[64:]
+            result[i * 8 + u] = x[:64] + x[64:]
+        out_copy(i).start()
         return 0
 
     lax.fori_loop(0, 4, some_rhs, 0)
+    for i in range(4):
+        out_copy(i).wait()
 
 
 UNROLL = 4
 
 
-def far_kernel(far, recv, cpl, gt_4, wt, near, out, sums, planes):
+def far_kernel(far, recv, gt_4, cpl_in, wt_in, near_in, out, cpl, wt, near, sums, planes, result, sems):
+    copies = [
+        pltpu.make_async_copy(source, target, sems.at[4 + i])
+        for i, (source, target) in enumerate([(cpl_in, cpl), (wt_in, wt), (near_in, near)])
+    ]
+    for copy in copies:
+        copy.start()
     lane_group = lax.broadcasted_iota(jnp.int32, (32, 128), 1) // 32
 
     def one_parent(c):
@@ -295,16 +314,20 @@
         x = x + pltpu.roll(x, 64, 1)
         sums[rows(c, 32), :] = x + pltpu.roll(x, 32, 1)
 
-    def some_parents(i, _):
-        for u in range(4):
-            one_parent(i * 4 + u)
-        return 0
-
-    lax.fori_loop(0, 4, some_parents, 0)
     packed = recv[0, pl.ds(INFLOW_AT, 8), :]
     for s in range(1, 16):
         packed = packed + recv[s, pl.ds(INFLOW_AT, 8), :]
     inflow_t = jnp.transpose(jnp.pad(unpack(packed), ((0, 96), (0, 96))))[:32, :32]
+
+    copies[0].wait()
+
+    def some_parents(i, _):
+        for u in range(8):
+            one_parent(i * 8 + u)
+        return 0
+
+    lax.fori_loop(0, 2, some_parents, 0)
+    copies[1].wait()
 
     def four_parents(i, _):
         x = jnp.transpose(sums[rows(i, 128), :])[:32] + dot3(inflow_t, gt_4[i], NN)
@@ -319,18 +342,31 @@
 
     lax.fori_loop(0, 4, four_parents, 0)
 
+    copies[2].wait()
+
+    def out_copy(i):
+        return pltpu.make_async_copy(result.at[pl.ds(i * 8, 8)], out.at[pl.ds(i * 8, 8)], sems.at[i])
+
     def some_rhs(i, _):
         for u in range(8):
             x = jnp.transpose(planes[i * 8 + u])
-            out[i * 8 + u] = x[:64] + x[64:] + near[i * 8 + u]
+            result[i * 8 + u] = x[:64] + x[64:] + near[i * 8 + u]
+        out_copy(i).start()
         return 0
 
     lax.fori_loop(0, 4, some_rhs, 0)
+    for i in range(4):
+        out_copy(i).wait()
 
 
 VMEM = pl.BlockSpec(memory_space=pltpu.VMEM)
 SMEM = pl.BlockSpec(memory_space=pltpu.SMEM)
 ANY = pl.BlockSpec(memory_space=pl.ANY)
+HBM = pl.BlockSpec(memory_space=pltpu.HBM)
+
+
+def in_hbm(x):
+    return pltpu.with_memory_space_constraint(x, pltpu.HBM)
 
 
 def f32(*shape):
@@ -382,7 +418,7 @@
             pltpu.SemaphoreType.DMA((18,)),
         ],
         out_specs=(ANY,) * 3,
-    )(send_list, sources, coords)
+    )(send_list, coords, sources)
     recv = lax.all_to_all(payload, "sub", 0, 0, tiled=True)
     wt, skel, own, gt_4 = call(
         upward_kernel,
@@ -418,25 +454,39 @@
     near = call(
         near_kernel,
         "near",
-        f32(32, 64, 128),
-        [SMEM] * 2 + [VMEM] * 2 + [ANY] * 2,
+        pltpu.HBM((32, 64, 128), F32),
+        [SMEM] * 2 + [VMEM] + [HBM] * 3,
         [
             pltpu.VMEM((385 * 32, 128), F32),
             pltpu.VMEM((385 * 8, 128), F32),
+            pltpu.VMEM((128, 64, 48), BF16),
             pltpu.VMEM((4096, 128), F32),
             planes,
+            pltpu.VMEM((32, 64, 128), F32),
             pltpu.VMEM((UNROLL, 64, 512), F32),
             pltpu.VMEM((UNROLL, 64, 512), F32),
-            pltpu.SemaphoreType.DMA((2,)),
+            pltpu.SemaphoreType.DMA((7,)),
         ],
-    )(near_list, near_count, recv, targets, src_t, feats)
+        mib=24,
+        out_specs=HBM,
+    )(near_list, near_count, recv, *[in_hbm(x) for x in (targets, src_t, feats)])
     return call(
         far_kernel,
         "far",
         f32(32, 64, 128),
-        [SMEM] + [VMEM] * 5,
-        [pltpu.VMEM((512, 128), F32), planes],
-    )(far_list, far_recv, cpl, gt_4, wt, near)
+        [SMEM] + [VMEM] * 2 + [HBM] * 3,
+        [
+            pltpu.VMEM((4, 512, 128), F32),
+            pltpu.VMEM((4096, 128), BF16),
+            pltpu.VMEM((32, 64, 128), F32),
+            pltpu.VMEM((512, 128), F32),
+            planes,
+            pltpu.VMEM((32, 64, 128), F32),
+            pltpu.SemaphoreType.DMA((7,)),
+        ],
+        mib=14,
+        out_specs=HBM,
+    )(far_list, far_recv, gt_4, *[in_hbm(x) for x in (cpl, wt, near)])
 
 
 def solution(mesh):

time: 77.8 us -> 75.4 us (0.969)
  Pallas kernels: 53.2 us -> 50.5 us
  waiting for transfers between devices: 5.46 us -> 6.72 us
  local copies, waits for them, and re-layouts: 1 us -> 0.02 us
    pallas_call x2, Pallas kernels: 25.7 us -> 23.1 us  [the longest x1 16.2 us: body(): call(near_kernel, 'near', pltpu.HBM((32, 64, 128), F32), [SMEM] * 2 + [VM...]
    all_to_all x1, waiting for transfers between devices: 0.64 us -> 1.93 us  [body(): far_recv = lax.all_to_all(far_payload, 'sub', 0, 0, tiled=True)]
    unnamed x6 -> x10, local copies, waits for them, and re-layouts: 1 us -> 0.02 us
where the time goes in v2:
time: 75.4 us; the launch traced here: 75 us
  Pallas kernels  50.5 us (67%)
  starting transfers between devices  16.4 us (22%)
  waiting for transfers between devices  6.72 us (9%)
  other arithmetic  1.3 us (2%)
    pallas_call x1, Pallas kernels, body(): call(near_kernel, 'near', pltpu.HBM((32, 64, 128), F32), [SMEM] * 2 + [VM...  16.2 us
    pallas_call x1, Pallas kernels, body(): call(upward_kernel, 'upward', (b16(4096, 128), f32(128, 128), f32(8, 128)...  9.66 us
    all_to_all x1, starting transfers between devices, body(): recv = lax.all_to_all(payload, 'sub', 0, 0, tiled=True)  8 us
    pallas_call x1, Pallas kernels, body(): call(far_kernel, 'far', f32(32, 64, 128), [SMEM] + [VMEM] * 2 + [HBM] * 3...  6.91 us
    pallas_call x1, Pallas kernels, body(): call(couple_kernel, 'couple', f32(4, 512, 128), [VMEM])  5.76 us
    pallas_call x1, Pallas kernels, body(): call(pack_kernel, 'pack', (f32(16, NEAR_ROWS, 128), f32(4096, 128), f32(1...  5.14 us
    ppermute x3, starting transfers between devices, body(): other = lax.ppermute(parts, 'grp', [(i, i ^ step) for i in range(8)])  4.55 us
    pallas_call x1, Pallas kernels, body(): call(own_kernel, 'own', (f32(1024, 128), b16(128, 64, 48)), [VMEM])(pts_t)  4.35 us
  transfers between devices with their start and end apart: 5, of which 3 were waited for; matrix products, arithmetic and copies ran while one was open for 2% of the time, Pallas kernels for 51%

profile of v2, /device:TPU:0, one launch (start us, length us, event | category | flops | bytes accessed | tf_op | source)
XLA Modules:
  0.0 75.0 jit_solution(132560307976413349)
XLA Ops:
  0.0 5.1 %pack.1 = (f32[16,280,128]{2,1,0:T(8,128)}, f32[4096,128]{1,0:T(8,128)}, f32[1024,128]{1,0:T(8,128)}) custom-call(s32[16,16]{1,0:T(8,128)} %send.1, f32[3,64,128]{2,1,0:T(8,128)} %crd.1, f32[32,64,128]{2,1,0:T(8,128)} %src.1), custom_call_target="tpu_custom_call" | custom-call | flops 1000000000 | bytes 4194304 | tf_op jit(solution)/shard_map/pack/pallas_call | solution.py:408
  5.2 8.0 %all-to-all-start = ((f32[16,280,128]{2,1,0:T(8,128)}), f32[16,280,128]{2,1,0:T(8,128)S(1)}, u32[]{:S(2)}, u32[]{:S(2)}) async-start(f32[16,280,128]{2,1,0:T(8,128)} %get-tuple-element.19), calls=%async_computation | async-start | bytes 4587520 | tf_op jit(solution)/shard_map/all_to_all | solution.py:422
  13.2 9.7 %upward.1 = (bf16[4096,128]{1,0:T(8,128)(2,1)}, f32[128,128]{1,0:T(8,128)}, f32[8,128]{1,0:T(8,128)}, f32[4,32,128]{2,1,0:T(8,128)}) custom-call(f32[4096,128]{1,0:T(8,128)} %get-tuple-element.20.src_t.vals_own, f32[32,64,128]{2,1,0:T(8,128)} %bas.1, f32[32,32,128]{2,1,0:T(8,128)} %tra.1, f32[32,16,32]{2,1,0:T(8,128)} %bitcast.7), custom_call_target="tpu_custom_call" | custom-call | flops 1000000000 | bytes 4194304 | tf_op jit(solution)/shard_map/upward/pallas_call | solution.py:423
  22.8 0.0 collective-permute-start
  22.8 1.4 %collective-permute-done = f32[1,8,128]{2,1,0:T(8,128)S(1)} collective-permute-done((f32[1,8,128]{2,1,0:T(8,128)}, f32[1,8,128]{2,1,0:T(8,128)S(1)}, u32[]{:S(2)}, u32[]{:S(2)}) %collective-permute-start) | collective-permute-done | bytes 4128 | tf_op jit(solution)/shard_map/ppermute | solution.py:432
  24.2 0.7 pad_maximum_fusion.2
  24.9 1.6 %collective-permute-start.1 = (f32[2,8,128]{2,1,0:T(8,128)S(1)}, f32[2,8,128]{2,1,0:T(8,128)S(1)}, u32[]{:S(2)}, u32[]{:S(2)}) collective-permute-start(f32[2,8,128]{2,1,0:T(8,128)S(1)} %pad_maximum_fusion.2), channel_id=1, source_target_pairs={{0,32},{16,48},{32,0},{48,16},{64,96},{80,112},{96,64},{112,80},{1... | collective-permute-start | bytes 24584 | tf_op jit(solution)/shard_map/ppermute | solution.py:432
  26.5 0.0 copy-start.4
  26.5 5.8 %couple.1.cpl_in = f32[4,512,128]{2,1,0:T(8,128)} custom-call(f32[32,16,16,32]{3,2,1,0:T(8,128)} %bitcast.5), custom_call_target="tpu_custom_call" | custom-call | flops 1000000000 | bytes 4194304 | tf_op jit(solution)/shard_map/couple/pallas_call | solution.py:450
  32.2 0.0 collective-permute-done.1
  32.2 0.0 copy-done.4
  32.2 3.0 %collective-permute-start.2 = (f32[4,8,128]{2,1,0:T(8,128)S(1)}, f32[4,8,128]{2,1,0:T(8,128)S(1)}, u32[]{:S(2)}, u32[]{:S(2)}) collective-permute-start(f32[4,8,128]{2,1,0:T(8,128)S(1)} %pad_maximum_fusion.1), channel_id=1, source_target_pairs={{0,64},{16,80},{32,96},{48,112},{64,0},{80,16},{96,32},{112,48},{1... | collective-permute-start | bytes 49160 | tf_op jit(solution)/shard_map/ppermute | solution.py:432
  35.2 4.4 %own.1 = (f32[1024,128]{1,0:T(8,128)}, bf16[128,64,48]{2,1,0:T(8,128)(2,1)}) custom-call(f32[1024,128]{1,0:T(8,128)} %get-tuple-element.23.pts_t), custom_call_target="tpu_custom_call" | custom-call | flops 1000000000 | bytes 4194304 | tf_op jit(solution)/shard_map/own/pallas_call | solution.py:451
  39.6 0.0 collective-permute-done.2
  39.6 0.6 pad_maximum_fusion.parts
  40.2 0.0 copy-start.2
  40.2 0.0 copy-start.3
  40.2 2.4 %inflow.1 = f32[16,136,128]{2,1,0:T(8,128)} custom-call(s32[1]{0:T(128)} %bitcast.group, f32[32,8,8,32]{3,2,1,0:T(8,128)} %bitcast.6, f32[8,8,128]{2,1,0:T(8,128)} %pad_maximum_fusion.parts, f32[128,128]{1,0:T(8,128)} %get-tuple-element.22.skel), custom_call_target="tpu_custom_call" | custom-call | tf_op jit(solution)/shard_map/inflow/pallas_call | solution.py:435
  42.6 3.4 %all-to-all-done.recv = f32[16,280,128]{2,1,0:T(8,128)S(1)} async-done(((f32[16,280,128]{2,1,0:T(8,128)}), f32[16,280,128]{2,1,0:T(8,128)S(1)}, u32[]{:S(2)}, u32[]{:S(2)}) %all-to-all-start) | async-done | bytes 2293792 | tf_op jit(solution)/shard_map/all_to_all | solution.py:422
  46.0 3.8 %all-to-all-start.1 = ((f32[16,136,128]{2,1,0:T(8,128)}), f32[16,136,128]{2,1,0:T(8,128)S(1)}, u32[]{:S(2)}, u32[]{:S(2)}) async-start(f32[16,136,128]{2,1,0:T(8,128)} %inflow.1), calls=%async_computation.1 | async-start | bytes 2228224 | tf_op jit(solution)/shard_map/all_to_all | solution.py:453
  49.9 0.0 copy-done.2
  49.9 0.0 copy-done.3
  49.9 0.0 copy-start
  49.9 0.0 copy-start.1
  49.9 16.2 %near.2.near_in = f32[32,64,128]{2,1,0:T(8,128)} custom-call(s32[7,128]{1,0:T(8,128)S(1)} %copy-done.2, s32[128]{0:T(128)S(1)} %copy-done.3, f32[16,280,128]{2,1,0:T(8,128)S(1)} %all-to-all-done.recv, bf16[128,64,48]{2,1,0:T(8,128)(2,1)} %get-tuple-element.31.targets_in, f32[4096,128]{1,0:T(8,128)} %get-tuple-element.20.src_t.vals_own, ...), custom_call_target="tpu_custom_call" | custom-call | flops 1000000000 | bytes 4194304 | tf_op jit(solution)/shard_map/near/pallas_call | solution.py:454
  66.1 1.9 %all-to-all-done.1.recv = f32[16,136,128]{2,1,0:T(8,128)S(1)} async-done(((f32[16,136,128]{2,1,0:T(8,128)}), f32[16,136,128]{2,1,0:T(8,128)S(1)}, u32[]{:S(2)}, u32[]{:S(2)}) %all-to-all-start.1) | async-done | bytes 1114144 | tf_op jit(solution)/shard_map/all_to_all | solution.py:453
  68.1 0.0 copy-done
  68.1 0.0 copy-done.1
  68.1 6.9 %far.2 = f32[32,64,128]{2,1,0:T(8,128)} custom-call(s32[16,16]{1,0:T(8,128)S(1)} %copy-done.1, f32[16,136,128]{2,1,0:T(8,128)S(1)} %all-to-all-done.1.recv, f32[4,32,128]{2,1,0:T(8,128)S(1)} %copy-done, f32[4,512,128]{2,1,0:T(8,128)} %couple.1.cpl_in, bf16[4096,128]{1,0:T(8,128)(2,1)} %get-tuple-element.29.wt_in, f32[32,64,128]{2,1,0:T(8,128)} %near.2.near_in), custom_call_target="tpu_custom_call" | custom-call | flops 1000000000 | bytes 4194304 | tf_op jit(solution)/shard_map/far/pallas_call | solution.py:473
  (1 shorter events, 0.0 us)
Async XLA Ops:
  5.2 40.9 %all-to-all-start = ((f32[16,280,128]{2,1,0:T(8,128)}), f32[16,280,128]{2,1,0:T(8,128)S(1)}, u32[]{:S(2)}, u32[]{:S(2)}) async-start(f32[16,280,128]{2,1,0:T(8,128)} %get-tuple-element.19), calls=%async_computation | async-start | bytes 4587520 | tf_op jit(solution)/shard_map/all_to_all | solution.py:422
  22.8 1.4 %collective-permute-start = (f32[1,8,128]{2,1,0:T(8,128)}, f32[1,8,128]{2,1,0:T(8,128)S(1)}, u32[]{:S(2)}, u32[]{:S(2)}) collective-permute-start(f32[1,8,128]{2,1,0:T(8,128)} %bitcast.8), channel_id=1, source_target_pairs={{0,16},{16,0},{32,48},{48,32},{64,80},{80,64},{96,112},{112,96},{1... | collective-permute-start | bytes 12296 | tf_op jit(solution)/shard_map/ppermute | solution.py:432
  24.9 7.3 %collective-permute-start.1 = (f32[2,8,128]{2,1,0:T(8,128)S(1)}, f32[2,8,128]{2,1,0:T(8,128)S(1)}, u32[]{:S(2)}, u32[]{:S(2)}) collective-permute-start(f32[2,8,128]{2,1,0:T(8,128)S(1)} %pad_maximum_fusion.2), channel_id=1, source_target_pairs={{0,32},{16,48},{32,0},{48,16},{64,96},{80,112},{96,64},{112,80},{1... | collective-permute-start | bytes 24584 | tf_op jit(solution)/shard_map/ppermute | solution.py:432
  26.5 5.8 %copy-start.4 = (f32[8,128]{1,0:T(8,128)S(1)}, f32[8,128]{1,0:T(8,128)}, u32[]{:S(2)}) copy-start(f32[8,128]{1,0:T(8,128)} %get-tuple-element.21) | copy-start | bytes 12292
  32.2 7.3 %collective-permute-start.2 = (f32[4,8,128]{2,1,0:T(8,128)S(1)}, f32[4,8,128]{2,1,0:T(8,128)S(1)}, u32[]{:S(2)}, u32[]{:S(2)}) collective-permute-start(f32[4,8,128]{2,1,0:T(8,128)S(1)} %pad_maximum_fusion.1), channel_id=1, source_target_pairs={{0,64},{16,80},{32,96},{48,112},{64,0},{80,16},{96,32},{112,48},{1... | collective-permute-start | bytes 49160 | tf_op jit(solution)/shard_map/ppermute | solution.py:432
  40.2 9.7 %copy-start.2 = (s32[7,128]{1,0:T(8,128)S(1)}, s32[7,128]{1,0:T(8,128)}, u32[]{:S(2)}) copy-start(s32[7,128]{1,0:T(8,128)} %near.3) | copy-start | bytes 10756
  40.2 9.7 %copy-start.3 = (s32[128]{0:T(128)S(1)}, s32[128]{0:T(128)}, u32[]{:S(2)}) copy-start(s32[128]{0:T(128)} %count.1) | copy-start | bytes 1540
  46.0 22.0 %all-to-all-start.1 = ((f32[16,136,128]{2,1,0:T(8,128)}), f32[16,136,128]{2,1,0:T(8,128)S(1)}, u32[]{:S(2)}, u32[]{:S(2)}) async-start(f32[16,136,128]{2,1,0:T(8,128)} %inflow.1), calls=%async_computation.1 | async-start | bytes 2228224 | tf_op jit(solution)/shard_map/all_to_all | solution.py:453
  49.9 18.2 %copy-start = (f32[4,32,128]{2,1,0:T(8,128)S(1)}, f32[4,32,128]{2,1,0:T(8,128)}, u32[]{:S(2)}) copy-start(f32[4,32,128]{2,1,0:T(8,128)} %get-tuple-element.27.gt_4) | copy-start | bytes 196612
  49.9 18.2 %copy-start.1 = (s32[16,16]{1,0:T(8,128)S(1)}, s32[16,16]{1,0:T(8,128)}, u32[]{:S(2)}) copy-start(s32[16,16]{1,0:T(8,128)} %far.3) | copy-start | bytes 3076

commit v3 on v2

--- a/solution.py
+++ b/solution.py
@@ -59,10 +59,14 @@
 
     lax.fori_loop(0, 4, source_rows, 0)
 
+    def source_copy(i):
+        return pltpu.make_async_copy(src_t.at[rows(i, 512), :], src_out.at[rows(i, 512), :], sems.at[17 + i])
+
     def eight_leaves(i, _):
         for g in (2 * i, 2 * i + 1):
             block = jnp.transpose(planes[:, rows(g, 8), :], (1, 0, 2))
             src_t[rows(g, 256), :] = block.reshape(256, 128)
+        source_copy(i).start()
         return 0
 
     lax.fori_loop(0, 8, eight_leaves, 0)
@@ -79,9 +83,8 @@
         return 0
 
     lax.fori_loop(0, 4, eight_points, 0)
-    copies = [pltpu.make_async_copy(src_t, src_out, sems.at[16]), pltpu.make_async_copy(pts_t, pts_out, sems.at[17])]
-    for copy in copies:
-        copy.start()
+    points_copy = pltpu.make_async_copy(pts_t, pts_out, sems.at[16])
+    points_copy.start()
     low = low_half((32, 128))
     low8 = low_half((8, 128))
 
@@ -99,7 +102,7 @@
         return 0
 
     lax.fori_loop(0, 8, two_peers, 0)
-    for copy in copies + [block_copy(q) for q in range(16)]:
+    for copy in [points_copy] + [source_copy(i) for i in range(8)] + [block_copy(q) for q in range(16)]:
         copy.wait()
 
 
@@ -297,8 +300,7 @@
         pltpu.make_async_copy(source, target, sems.at[4 + i])
         for i, (source, target) in enumerate([(cpl_in, cpl), (wt_in, wt), (near_in, near)])
     ]
-    for copy in copies:
-        copy.start()
+    copies[0].start()
     lane_group = lax.broadcasted_iota(jnp.int32, (32, 128), 1) // 32
 
     def one_parent(c):
@@ -320,6 +322,8 @@
     inflow_t = jnp.transpose(jnp.pad(unpack(packed), ((0, 96), (0, 96))))[:32, :32]
 
     copies[0].wait()
+    copies[1].start()
+    copies[2].start()
 
     def some_parents(i, _):
         for u in range(8):
@@ -334,9 +338,11 @@
         field = jnp.concatenate(split(x), 0)
         for u in range(4):
             leaves = []
-            for v in range(8):
-                acc = mm(field[:, 32 * u : 32 * u + 32], wt[rows(i * 32 + u * 8 + v, 32), :], NN)
-                leaves.append(acc[:32] + acc[32:])
+            for v in range(0, 8, 2):
+                both = [wt[rows(i * 32 + u * 8 + v + w, 32), :] for w in (0, 1)]
+                acc = mm(field[:, 32 * u : 32 * u + 32], jnp.concatenate(both, 1), NN)
+                acc = acc[:32] + acc[32:]
+                leaves += [acc[:, :128], acc[:, 128:]]
             planes[:, rows(i * 4 + u, 8), :] = jnp.transpose(jnp.stack(leaves, 0), (1, 0, 2))
         return 0
 
@@ -415,7 +421,7 @@
             pltpu.VMEM((1024, 128), F32),
             planes,
             pltpu.VMEM((16, NEAR_ROWS, 128), F32),
-            pltpu.SemaphoreType.DMA((18,)),
+            pltpu.SemaphoreType.DMA((25,)),
         ],
         out_specs=(ANY,) * 3,
     )(send_list, coords, sources)

time: 75.4 us -> 74.7 us (level)
  transfers between devices with their start and end apart: 5 -> 5, of which waited for: 3 -> 3; matrix products, arithmetic and copies ran while one was open for 2% -> 2% of each run, Pallas kernels for 51% -> 52%
where the time goes in v3:
time: 74.7 us; the launch traced here: 74.3 us
  Pallas kernels  49.8 us (67%)
  starting transfers between devices  16.4 us (22%)
  waiting for transfers between devices  6.74 us (9%)
  other arithmetic  1.3 us (2%)
    pallas_call x1, Pallas kernels, body(): call(near_kernel, 'near', pltpu.HBM((32, 64, 128), F32), [SMEM] * 2 + [VM...  16.2 us
    pallas_call x1, Pallas kernels, body(): call(upward_kernel, 'upward', (b16(4096, 128), f32(128, 128), f32(8, 128)...  9.65 us
    all_to_all x1, starting transfers between devices, body(): recv = lax.all_to_all(payload, 'sub', 0, 0, tiled=True)  8 us
    pallas_call x1, Pallas kernels, body(): call(far_kernel, 'far', f32(32, 64, 128), [SMEM] + [VMEM] * 2 + [HBM] * 3...  6.75 us
    pallas_call x1, Pallas kernels, body(): call(couple_kernel, 'couple', f32(4, 512, 128), [VMEM])  5.76 us
    pallas_call x1, Pallas kernels, body(): call(pack_kernel, 'pack', (f32(16, NEAR_ROWS, 128), f32(4096, 128), f32(1...  4.58 us
    ppermute x3, starting transfers between devices, body(): other = lax.ppermute(parts, 'grp', [(i, i ^ step) for i in range(8)])  4.57 us
    pallas_call x1, Pallas kernels, body(): call(own_kernel, 'own', (f32(1024, 128), b16(128, 64, 48)), [VMEM])(pts_t)  4.35 us
  transfers between devices with their start and end apart: 5, of which 3 were waited for; matrix products, arithmetic and copies ran while one was open for 2% of the time, Pallas kernels for 52%

profile of v3, /device:TPU:0, one launch (start us, length us, event | category | flops | bytes accessed | tf_op | source)
XLA Modules:
  0.0 74.3 jit_solution(11279868581237046035)
XLA Ops:
  0.0 4.6 %pack.1 = (f32[16,280,128]{2,1,0:T(8,128)}, f32[4096,128]{1,0:T(8,128)}, f32[1024,128]{1,0:T(8,128)}) custom-call(s32[16,16]{1,0:T(8,128)} %send.1, f32[3,64,128]{2,1,0:T(8,128)} %crd.1, f32[32,64,128]{2,1,0:T(8,128)} %src.1), custom_call_target="tpu_custom_call" | custom-call | flops 1000000000 | bytes 4194304 | tf_op jit(solution)/shard_map/pack/pallas_call | solution.py:414
  4.6 8.0 %all-to-all-start = ((f32[16,280,128]{2,1,0:T(8,128)}), f32[16,280,128]{2,1,0:T(8,128)S(1)}, u32[]{:S(2)}, u32[]{:S(2)}) async-start(f32[16,280,128]{2,1,0:T(8,128)} %get-tuple-element.19), calls=%async_computation | async-start | bytes 4587520 | tf_op jit(solution)/shard_map/all_to_all | solution.py:428
  12.6 9.7 %upward.1 = (bf16[4096,128]{1,0:T(8,128)(2,1)}, f32[128,128]{1,0:T(8,128)}, f32[8,128]{1,0:T(8,128)}, f32[4,32,128]{2,1,0:T(8,128)}) custom-call(f32[4096,128]{1,0:T(8,128)} %get-tuple-element.20.src_t.vals_own, f32[32,64,128]{2,1,0:T(8,128)} %bas.1, f32[32,32,128]{2,1,0:T(8,128)} %tra.1, f32[32,16,32]{2,1,0:T(8,128)} %bitcast.7), custom_call_target="tpu_custom_call" | custom-call | flops 1000000000 | bytes 4194304 | tf_op jit(solution)/shard_map/upward/pallas_call | solution.py:429
  22.2 0.0 collective-permute-start
  22.3 1.4 %collective-permute-done = f32[1,8,128]{2,1,0:T(8,128)S(1)} collective-permute-done((f32[1,8,128]{2,1,0:T(8,128)}, f32[1,8,128]{2,1,0:T(8,128)S(1)}, u32[]{:S(2)}, u32[]{:S(2)}) %collective-permute-start) | collective-permute-done | bytes 4128 | tf_op jit(solution)/shard_map/ppermute | solution.py:438
  23.6 0.7 pad_maximum_fusion.2
  24.3 1.6 %collective-permute-start.1 = (f32[2,8,128]{2,1,0:T(8,128)S(1)}, f32[2,8,128]{2,1,0:T(8,128)S(1)}, u32[]{:S(2)}, u32[]{:S(2)}) collective-permute-start(f32[2,8,128]{2,1,0:T(8,128)S(1)} %pad_maximum_fusion.2), channel_id=1, source_target_pairs={{0,32},{16,48},{32,0},{48,16},{64,96},{80,112},{96,64},{112,80},{1... | collective-permute-start | bytes 24584 | tf_op jit(solution)/shard_map/ppermute | solution.py:438
  25.9 0.0 copy-start.4
  25.9 5.8 %couple.1.cpl_in = f32[4,512,128]{2,1,0:T(8,128)} custom-call(f32[32,16,16,32]{3,2,1,0:T(8,128)} %bitcast.5), custom_call_target="tpu_custom_call" | custom-call | flops 1000000000 | bytes 4194304 | tf_op jit(solution)/shard_map/couple/pallas_call | solution.py:456
  31.7 0.0 collective-permute-done.1
  31.7 0.0 copy-done.4
  31.7 3.0 %collective-permute-start.2 = (f32[4,8,128]{2,1,0:T(8,128)S(1)}, f32[4,8,128]{2,1,0:T(8,128)S(1)}, u32[]{:S(2)}, u32[]{:S(2)}) collective-permute-start(f32[4,8,128]{2,1,0:T(8,128)S(1)} %pad_maximum_fusion.1), channel_id=1, source_target_pairs={{0,64},{16,80},{32,96},{48,112},{64,0},{80,16},{96,32},{112,48},{1... | collective-permute-start | bytes 49160 | tf_op jit(solution)/shard_map/ppermute | solution.py:438
  34.7 4.4 %own.1 = (f32[1024,128]{1,0:T(8,128)}, bf16[128,64,48]{2,1,0:T(8,128)(2,1)}) custom-call(f32[1024,128]{1,0:T(8,128)} %get-tuple-element.23.pts_t), custom_call_target="tpu_custom_call" | custom-call | flops 1000000000 | bytes 4194304 | tf_op jit(solution)/shard_map/own/pallas_call | solution.py:457
  39.0 0.0 collective-permute-done.2
  39.0 0.6 pad_maximum_fusion.parts
  39.6 0.0 copy-start.2
  39.6 0.0 copy-start.3
  39.6 2.4 %inflow.1 = f32[16,136,128]{2,1,0:T(8,128)} custom-call(s32[1]{0:T(128)} %bitcast.group, f32[32,8,8,32]{3,2,1,0:T(8,128)} %bitcast.6, f32[8,8,128]{2,1,0:T(8,128)} %pad_maximum_fusion.parts, f32[128,128]{1,0:T(8,128)} %get-tuple-element.22.skel), custom_call_target="tpu_custom_call" | custom-call | tf_op jit(solution)/shard_map/inflow/pallas_call | solution.py:441
  42.1 3.4 %all-to-all-done.recv = f32[16,280,128]{2,1,0:T(8,128)S(1)} async-done(((f32[16,280,128]{2,1,0:T(8,128)}), f32[16,280,128]{2,1,0:T(8,128)S(1)}, u32[]{:S(2)}, u32[]{:S(2)}) %all-to-all-start) | async-done | bytes 2293792 | tf_op jit(solution)/shard_map/all_to_all | solution.py:428
  45.5 3.8 %all-to-all-start.1 = ((f32[16,136,128]{2,1,0:T(8,128)}), f32[16,136,128]{2,1,0:T(8,128)S(1)}, u32[]{:S(2)}, u32[]{:S(2)}) async-start(f32[16,136,128]{2,1,0:T(8,128)} %inflow.1), calls=%async_computation.1 | async-start | bytes 2228224 | tf_op jit(solution)/shard_map/all_to_all | solution.py:459
  49.3 0.0 copy-done.2
  49.3 0.0 copy-done.3
  49.3 0.0 copy-start
  49.3 0.0 copy-start.1
  49.3 16.2 %near.2.near_in = f32[32,64,128]{2,1,0:T(8,128)} custom-call(s32[7,128]{1,0:T(8,128)S(1)} %copy-done.2, s32[128]{0:T(128)S(1)} %copy-done.3, f32[16,280,128]{2,1,0:T(8,128)S(1)} %all-to-all-done.recv, bf16[128,64,48]{2,1,0:T(8,128)(2,1)} %get-tuple-element.31.targets_in, f32[4096,128]{1,0:T(8,128)} %get-tuple-element.20.src_t.vals_own, ...), custom_call_target="tpu_custom_call" | custom-call | flops 1000000000 | bytes 4194304 | tf_op jit(solution)/shard_map/near/pallas_call | solution.py:460
  65.6 2.0 %all-to-all-done.1.recv = f32[16,136,128]{2,1,0:T(8,128)S(1)} async-done(((f32[16,136,128]{2,1,0:T(8,128)}), f32[16,136,128]{2,1,0:T(8,128)S(1)}, u32[]{:S(2)}, u32[]{:S(2)}) %all-to-all-start.1) | async-done | bytes 1114144 | tf_op jit(solution)/shard_map/all_to_all | solution.py:459
  67.5 0.0 copy-done
  67.5 0.0 copy-done.1
  67.5 6.7 %far.2 = f32[32,64,128]{2,1,0:T(8,128)} custom-call(s32[16,16]{1,0:T(8,128)S(1)} %copy-done.1, f32[16,136,128]{2,1,0:T(8,128)S(1)} %all-to-all-done.1.recv, f32[4,32,128]{2,1,0:T(8,128)S(1)} %copy-done, f32[4,512,128]{2,1,0:T(8,128)} %couple.1.cpl_in, bf16[4096,128]{1,0:T(8,128)(2,1)} %get-tuple-element.29.wt_in, f32[32,64,128]{2,1,0:T(8,128)} %near.2.near_in), custom_call_target="tpu_custom_call" | custom-call | flops 1000000000 | bytes 4194304 | tf_op jit(solution)/shard_map/far/pallas_call | solution.py:479
  (1 shorter events, 0.0 us)
Async XLA Ops:
  4.6 40.9 %all-to-all-start = ((f32[16,280,128]{2,1,0:T(8,128)}), f32[16,280,128]{2,1,0:T(8,128)S(1)}, u32[]{:S(2)}, u32[]{:S(2)}) async-start(f32[16,280,128]{2,1,0:T(8,128)} %get-tuple-element.19), calls=%async_computation | async-start | bytes 4587520 | tf_op jit(solution)/shard_map/all_to_all | solution.py:428
  22.2 1.4 %collective-permute-start = (f32[1,8,128]{2,1,0:T(8,128)}, f32[1,8,128]{2,1,0:T(8,128)S(1)}, u32[]{:S(2)}, u32[]{:S(2)}) collective-permute-start(f32[1,8,128]{2,1,0:T(8,128)} %bitcast.8), channel_id=1, source_target_pairs={{0,16},{16,0},{32,48},{48,32},{64,80},{80,64},{96,112},{112,96},{1... | collective-permute-start | bytes 12296 | tf_op jit(solution)/shard_map/ppermute | solution.py:438
  24.3 7.4 %collective-permute-start.1 = (f32[2,8,128]{2,1,0:T(8,128)S(1)}, f32[2,8,128]{2,1,0:T(8,128)S(1)}, u32[]{:S(2)}, u32[]{:S(2)}) collective-permute-start(f32[2,8,128]{2,1,0:T(8,128)S(1)} %pad_maximum_fusion.2), channel_id=1, source_target_pairs={{0,32},{16,48},{32,0},{48,16},{64,96},{80,112},{96,64},{112,80},{1... | collective-permute-start | bytes 24584 | tf_op jit(solution)/shard_map/ppermute | solution.py:438
  25.9 5.8 %copy-start.4 = (f32[8,128]{1,0:T(8,128)S(1)}, f32[8,128]{1,0:T(8,128)}, u32[]{:S(2)}) copy-start(f32[8,128]{1,0:T(8,128)} %get-tuple-element.21) | copy-start | bytes 12292
  31.7 7.3 %collective-permute-start.2 = (f32[4,8,128]{2,1,0:T(8,128)S(1)}, f32[4,8,128]{2,1,0:T(8,128)S(1)}, u32[]{:S(2)}, u32[]{:S(2)}) collective-permute-start(f32[4,8,128]{2,1,0:T(8,128)S(1)} %pad_maximum_fusion.1), channel_id=1, source_target_pairs={{0,64},{16,80},{32,96},{48,112},{64,0},{80,16},{96,32},{112,48},{1... | collective-permute-start | bytes 49160 | tf_op jit(solution)/shard_map/ppermute | solution.py:438
  39.6 9.7 %copy-start.2 = (s32[7,128]{1,0:T(8,128)S(1)}, s32[7,128]{1,0:T(8,128)}, u32[]{:S(2)}) copy-start(s32[7,128]{1,0:T(8,128)} %near.3) | copy-start | bytes 10756
  39.6 9.7 %copy-start.3 = (s32[128]{0:T(128)S(1)}, s32[128]{0:T(128)}, u32[]{:S(2)}) copy-start(s32[128]{0:T(128)} %count.1) | copy-start | bytes 1540
  45.5 22.0 %all-to-all-start.1 = ((f32[16,136,128]{2,1,0:T(8,128)}), f32[16,136,128]{2,1,0:T(8,128)S(1)}, u32[]{:S(2)}, u32[]{:S(2)}) async-start(f32[16,136,128]{2,1,0:T(8,128)} %inflow.1), calls=%async_computation.1 | async-start | bytes 2228224 | tf_op jit(solution)/shard_map/all_to_all | solution.py:459
  49.3 18.2 %copy-start = (f32[4,32,128]{2,1,0:T(8,128)S(1)}, f32[4,32,128]{2,1,0:T(8,128)}, u32[]{:S(2)}) copy-start(f32[4,32,128]{2,1,0:T(8,128)} %get-tuple-element.27.gt_4) | copy-start | bytes 196612
  49.3 18.2 %copy-start.1 = (s32[16,16]{1,0:T(8,128)S(1)}, s32[16,16]{1,0:T(8,128)}, u32[]{:S(2)}) copy-start(s32[16,16]{1,0:T(8,128)} %far.3) | copy-start | bytes 3076
